TPU v7x, 512 devices: a whole 4x8x8 slice. The times are simulated.
512 devices in a mesh: patch: 64 (over y, z), visit: 8 (over x, core).
Axes of the slice: x: 4, y: 8, z: 8, core: 2. Of those that a mesh axis runs over, the one named last changes fastest.
Arguments:
- stamps: bfloat16 [8, 8192, 32, 128], P('visit', 'patch'), may hold values from -6 to 6
- coefs: bfloat16 [8, 8192, 64], P('visit', 'patch'), may hold values from -0.75 to 0.75
- basis: bfloat16 [8, 64, 21, 21], P('visit', 'patch'), may hold values from -0.29882812 to 0.29882812
- taps: bfloat16 [8, 8192, 8], P('visit', 'patch'), may hold values from 0.049804688 to 0.59765625
- weights: bfloat16 [8, 8192], P('visit', 'patch'), may hold values from 0.19921875 to 5
- target: int32 [8, 8192, 1], P('visit', 'patch'), may hold values from 0 to 63; in each aligned block of 128 rows (0 to 127, 128 to 255, ..., all dimensions but the last counted through in order) at most 4 rows name the same one
- row_offset: int32 [8, 8192], P('visit', 'patch'), may hold values from 0 to 223
- col_offset: int32 [8, 8192], P('visit', 'patch'), may hold values from 0 to 127
Outputs:
- coadd: float32 [64, 256, 256], P('patch', 'visit')
- depth_map: float32 [64, 256, 256], P('patch', 'visit')
Inputs may be any that keep to these rules, and one draw needn't show every extreme that they name: `target`: among the rows of one device no patch is named more than 4 times, a bound that some block reaches.
All inputs are finite; a program needn't handle non-finite values.
Results may differ from a plain program's by a relative error of at most 0.0057.
Values may be sent and summed in bfloat16 or wider, within the bound.
No kernel may reach another device: no remote copies, remote signals or barrier semaphores. Data moves between devices by JAX's collectives and lax.ppermute only.
A program may use at most 64 MiB of HBM per device.

v0:
```python
import jax
import jax.numpy as jnp
from jax import lax
from jax.sharding import PartitionSpec as P

PATCH_ROWS = 256
PATCH_COLS = 256


def make_kernels(coefficients, basis_set):
    term_count = basis_set.shape[0]
    kernel_size = basis_set.shape[1]
    flat = jnp.dot(
        coefficients,
        basis_set.reshape(term_count, kernel_size * kernel_size),
        preferred_element_type=jnp.float32,
    )
    return flat.astype(jnp.bfloat16).reshape(coefficients.shape[0], kernel_size, kernel_size)


def convolve(pixels, kernels):
    kernel_size = kernels.shape[1]
    kernel_reach = kernel_size // 2
    height = pixels.shape[1]
    breadth = pixels.shape[2]
    padded = jnp.pad(pixels, ((0, 0), (0, 0), (kernel_reach, kernel_reach)))
    shifted = jnp.stack(
        [
            padded[:, :, column_shift : column_shift + breadth]
            for column_shift in range(kernel_size)
        ],
        axis=1,
    )
    offsets = (
        jnp.arange(height, dtype=jnp.int32)[None, :]
        - jnp.arange(height, dtype=jnp.int32)[:, None]
        + kernel_reach
    )
    onehot = (
        offsets[None, :, :] == jnp.arange(kernel_size, dtype=jnp.int32)[:, None, None]
    ).astype(jnp.bfloat16)
    toeplitz = jnp.einsum(
        "nab,aij->nbij", kernels, onehot, preferred_element_type=jnp.float32
    ).astype(jnp.bfloat16)
    result = jnp.einsum("nbik,nbkj->nij", toeplitz, shifted, preferred_element_type=jnp.float32)
    return result.astype(jnp.bfloat16)


def resample(convolved, tap_values, scale, row_start, col_start):
    height = convolved.shape[1]
    breadth = convolved.shape[2]
    column_gap = (
        jnp.arange(PATCH_COLS, dtype=jnp.int32)[None, :, None]
        - col_start[:, None, None]
        - jnp.arange(breadth, dtype=jnp.int32)[None, None, :]
        + 1
    )
    row_gap = (
        jnp.arange(PATCH_ROWS, dtype=jnp.int32)[None, :, None]
        - row_start[:, None, None]
        - jnp.arange(height, dtype=jnp.int32)[None, None, :]
        + 1
    )
    column_sum = jnp.zeros(column_gap.shape, jnp.float32)
    row_sum = jnp.zeros(row_gap.shape, jnp.float32)
    for tap_index in range(4):
        column_sum = column_sum + jnp.where(
            column_gap == tap_index,
            tap_values[:, 4 + tap_index].astype(jnp.float32)[:, None, None],
            0.0,
        )
        row_sum = row_sum + jnp.where(
            row_gap == tap_index, tap_values[:, tap_index].astype(jnp.float32)[:, None, None], 0.0
        )
    column_map = column_sum.astype(jnp.bfloat16)
    row_map = (scale.astype(jnp.float32)[:, None, None] * row_sum).astype(jnp.bfloat16)
    spread = jnp.einsum(
        "nij,ncj->nic", convolved, column_map, preferred_element_type=jnp.float32
    ).astype(jnp.bfloat16)
    return (row_map, column_map, spread)


def accumulate(pixels, extras, starts, full_basis):
    block_size = 8
    block_count = pixels.shape[0] // block_size
    term_count = full_basis.shape[0]
    blocks = (
        pixels.reshape(block_count, block_size, pixels.shape[1], pixels.shape[2]),
        extras.reshape(block_count, block_size, extras.shape[1]),
        starts.reshape(block_count, block_size, 2),
    )

    def update(state, block):
        numerator, depth_map = state
        convolved, extra_block, start_block = block
        convolved = convolve(convolved, make_kernels(extra_block[:, :term_count], full_basis))
        extra_block = extra_block[:, term_count:]
        row_map, column_map, spread = resample(
            convolved, extra_block[:, :8], extra_block[:, 8], start_block[:, 0], start_block[:, 1]
        )
        numerator = numerator + jnp.einsum(
            "nri,nic->rc", row_map, spread, preferred_element_type=jnp.float32
        )
        row_weight = jnp.sum(row_map.astype(jnp.float32), axis=2)
        column_weight = jnp.sum(column_map.astype(jnp.float32), axis=2)
        depth_map = depth_map + jnp.dot(
            row_weight.T, column_weight, precision=lax.Precision.HIGHEST
        )
        return ((numerator, depth_map), None)

    initial = (
        jnp.zeros((PATCH_ROWS, PATCH_COLS), jnp.float32),
        jnp.zeros((PATCH_ROWS, PATCH_COLS), jnp.float32),
    )
    final_state, unused = lax.scan(update, initial, blocks)
    return final_state


def per_device(stamps, coefs, basis, taps, weights, target, row_offset, col_offset):
    peer_count = lax.axis_size("patch")
    stamp_count = stamps.shape[1]
    height = stamps.shape[2]
    breadth = stamps.shape[3]
    slot_count = 2 * stamp_count // peer_count
    full_basis = lax.all_gather(basis[0], "patch", axis=0, tiled=True)
    destination = target[0, :, 0]
    position = jnp.arange(stamp_count, dtype=jnp.int32)
    earlier = (destination[None, :] == destination[:, None]) & (
        position[None, :] < position[:, None]
    )
    standing = jnp.sum(earlier.astype(jnp.int32), axis=1)
    placement = destination * slot_count + standing
    chooser = placement[None, :] == jnp.arange(peer_count * slot_count, dtype=jnp.int32)[:, None]
    select = chooser.astype(jnp.bfloat16)

    def pack(values):
        packed = jnp.dot(select, values, preferred_element_type=jnp.float32).astype(jnp.bfloat16)
        return packed.reshape(peer_count, slot_count, values.shape[1])

    starts = jnp.stack([row_offset[0], col_offset[0]], axis=1)
    packed_starts = jnp.sum(jnp.where(chooser[:, :, None], starts[None, :, :], 0), axis=1).reshape(
        peer_count, slot_count, 2
    )
    total_slots = peer_count * slot_count
    extras = jnp.concatenate([coefs[0], taps[0], weights[0][:, None]], axis=1)
    packed_pixels = pack(stamps[0].reshape(stamp_count, height * breadth))
    packed_extras = pack(extras)
    got_pixels, got_extras, got_starts = (
        lax.all_to_all(packed_pixels, "patch", split_axis=0, concat_axis=0, tiled=True),
        lax.all_to_all(packed_extras, "patch", split_axis=0, concat_axis=0, tiled=True),
        lax.all_to_all(packed_starts, "patch", split_axis=0, concat_axis=0, tiled=True),
    )
    numerator, depth_map = accumulate(
        got_pixels.reshape(total_slots, height, breadth),
        got_extras.reshape(total_slots, got_extras.shape[2]),
        got_starts.reshape(total_slots, 2),
        full_basis,
    )
    numerator, depth_map = (
        lax.psum_scatter(numerator, "visit", scatter_dimension=0, tiled=True),
        lax.psum_scatter(depth_map, "visit", scatter_dimension=0, tiled=True),
    )
    coadd = numerator / (1.0 + depth_map)
    return (coadd[None], depth_map[None])


def solution(mesh):
    placed = (
        P("visit", "patch", None, None),
        P("visit", "patch", None),
        P("visit", "patch", None, None),
        P("visit", "patch", None),
        P("visit", "patch"),
        P("visit", "patch", None),
        P("visit", "patch"),
        P("visit", "patch"),
    )
    return jax.shard_map(
        per_device,
        mesh=mesh,
        in_specs=placed,
        out_specs=(P("patch", "visit", None), P("patch", "visit", None)),
        check_vma=False,
    )
```

profile of v0, /device:TPU:1, one launch (start us, length us, event | category | flops | bytes accessed | tf_op | source)
XLA Modules:
  0.0 502.3 jit_solution(15867285318595806077)
XLA Ops:
  7.2 0.9 convert_reduce_fusion.2
  10.4 17.1 %all-to-all-start.1 = ((s32[64,4,2]{1,2,0:T(2,128)}), s32[64,4,2]{1,2,0:T(2,128)S(1)}, u32[]{:S(2)}, u32[]{:S(2)}) async-start(s32[64,4,2]{1,2,0:T(2,128)} %copy.93), calls=%async_computation.1 | async-start | bytes 131072 | tf_op jit(solution)/shard_map/all_to_all | solution.py:151
  27.5 2.0 convolution_convert_fusion.3
  29.5 2.2 reshape.221
  31.7 6.9 %all-to-all-done.1 = s32[64,4,2]{1,2,0:T(2,128)S(1)} async-done(((s32[64,4,2]{1,2,0:T(2,128)}), s32[64,4,2]{1,2,0:T(2,128)S(1)}, u32[]{:S(2)}, u32[]{:S(2)}) %all-to-all-start.1) | async-done | bytes 2080 | tf_op jit(solution)/shard_map/all_to_all | solution.py:151
  38.6 5.4 %all-to-all-start.2 = ((bf16[64,4,4096]{2,1,0:T(4,128)(2,1)}), bf16[64,4,4096]{2,1,0:T(4,128)(2,1)S(1)}, u32[]{:S(2)}, u32[]{:S(2)}) async-start(bf16[64,4,4096]{2,1,0:T(4,128)(2,1)} %reshape.221), calls=%async_computation.2 | async-start | bytes 4194304 | tf_op jit(solution)/shard_map/all_to_all | solution.py:149
  45.0 47.8 %all-to-all-done.2 = bf16[64,4,4096]{2,1,0:T(4,128)(2,1)S(1)} async-done(((bf16[64,4,4096]{2,1,0:T(4,128)(2,1)}), bf16[64,4,4096]{2,1,0:T(4,128)(2,1)S(1)}, u32[]{:S(2)}, u32[]{:S(2)}) %all-to-all-start.2) | async-done | bytes 2097184 | tf_op jit(solution)/shard_map/all_to_all | solution.py:149
  92.7 14.6 %all-to-all-start = ((bf16[64,4,73]{2,1,0:T(4,128)(2,1)}), bf16[64,4,73]{2,1,0:T(4,128)(2,1)S(1)}, u32[]{:S(2)}, u32[]{:S(2)}) async-start(bf16[64,4,73]{2,1,0:T(4,128)(2,1)} %bitcast.4), calls=%async_computation | async-start | bytes 131072 | tf_op jit(solution)/shard_map/all_to_all | solution.py:150
  107.4 38.0 %all-gather = bf16[64,1,21,21]{3,2,1,0:T(8,128)(2,1)S(1)} all-gather(bf16[1,1,21,21]{3,2,1,0:T(8,128)(2,1)S(1)} %copy-done.3), channel_id=2, replica_groups=mesh['patch'=64,'visit'=8] {'patch'}, dimensions={0}, use_global_device_ids=true | all-gather | bytes 57330 | tf_op jit(solution)/shard_map/all_gather | solution.py:125
  145.9 3.2 reshape_reshape.11
  149.1 261.2 %while.16 = (s32[]{:T(128)}, f32[256,256]{1,0:T(8,128)S(1)}, f32[256,256]{1,0:T(8,128)S(1)}, bf16[32,8,73]{2,1,0:T(8,128)(2,1)S(1)}, s32[32,8,2]{1,0,2:T(8,128)S...) while((s32[]{:T(128)}, f32[256,256]{1,0:T(8,128)S(1)}, ...), condition=%wide.wide.region_5.6_spmd.clone, body=%wide.wide.region_2.5_spmd.clone.sunk | while | flops 118861328 | bytes 6383152 | solution.py:115
  151.0 0.9 bitcast_dynamic-update-slice_fusion.3
  154.7 0.9 fusion.192
  159.2 0.9 bitcast_dynamic-update-slice_fusion.3
  162.9 0.9 fusion.192
  167.3 0.9 bitcast_dynamic-update-slice_fusion.3
  171.0 0.9 fusion.192
  175.5 0.9 bitcast_dynamic-update-slice_fusion.3
  179.2 0.9 fusion.192
  183.7 0.9 bitcast_dynamic-update-slice_fusion.3
  187.4 0.9 fusion.192
  191.8 0.9 bitcast_dynamic-update-slice_fusion.3
  195.5 0.9 fusion.192
  200.0 0.9 bitcast_dynamic-update-slice_fusion.3
  203.7 0.9 fusion.192
  208.2 0.9 bitcast_dynamic-update-slice_fusion.3
  211.9 0.9 fusion.192
  216.3 0.9 bitcast_dynamic-update-slice_fusion.3
  220.0 0.9 fusion.192
  224.5 0.9 bitcast_dynamic-update-slice_fusion.3
  228.2 0.9 fusion.192
  232.7 0.9 bitcast_dynamic-update-slice_fusion.3
  236.4 0.9 fusion.192
  240.8 0.9 bitcast_dynamic-update-slice_fusion.3
  244.5 0.9 fusion.192
  249.0 0.9 bitcast_dynamic-update-slice_fusion.3
  252.7 0.9 fusion.192
  257.1 0.9 bitcast_dynamic-update-slice_fusion.3
  260.9 0.9 fusion.192
  265.3 0.9 bitcast_dynamic-update-slice_fusion.3
  269.0 0.9 fusion.192
  273.5 0.9 bitcast_dynamic-update-slice_fusion.3
  277.2 0.9 fusion.192
  281.6 0.9 bitcast_dynamic-update-slice_fusion.3
  285.3 0.9 fusion.192
  289.8 0.9 bitcast_dynamic-update-slice_fusion.3
  293.5 0.9 fusion.192
  301.7 0.9 fusion.192
  309.8 0.9 fusion.192
  318.0 0.9 fusion.192
  326.2 0.9 fusion.192
  334.3 0.9 fusion.192
  342.5 0.9 fusion.192
  350.7 0.9 fusion.192
  358.8 0.9 fusion.192
  367.0 0.9 fusion.192
  375.2 0.9 fusion.192
  383.3 0.9 fusion.192
  391.5 0.9 fusion.192
  399.6 0.9 fusion.192
  407.8 0.9 fusion.192
  411.8 44.5 %reduce-scatter.5.cloned.1.call-done = f32[32,256]{1,0:T(8,128)} async-done(((f32[256,256]{1,0:T(8,128)}), f32[32,256]{1,0:T(8,128)}) %reduce-scatter.5.cloned.1.call-update) | async-done | bytes 32784 | tf_op jit(solution)/shard_map/reduce_scatter | solution.py:161
  456.3 37.8 %reduce-scatter.3.cloned.1.call-done = f32[32,256]{1,0:T(8,128)} async-done(((f32[256,256]{1,0:T(8,128)}), f32[32,256]{1,0:T(8,128)}) %reduce-scatter.3.cloned.1.call-update) | async-done | bytes 32784 | tf_op jit(solution)/shard_map/reduce_scatter | solution.py:160
  494.1 1.4 divide_bitcast_fusion
  (1167 shorter events, 216.5 us)
Async XLA Ops:
  10.4 28.3 %all-to-all-start.1 = ((s32[64,4,2]{1,2,0:T(2,128)}), s32[64,4,2]{1,2,0:T(2,128)S(1)}, u32[]{:S(2)}, u32[]{:S(2)}) async-start(s32[64,4,2]{1,2,0:T(2,128)} %copy.93), calls=%async_computation.1 | async-start | bytes 131072 | tf_op jit(solution)/shard_map/all_to_all | solution.py:151
  31.7 12.3 %copy-start.4 = (bf16[1,128,64]{1,2,0:T(8,128)(2,1)S(1)}, bf16[1,128,64]{1,2,0:T(8,128)(2,1)}, u32[]{:S(2)}) copy-start(bf16[1,128,64]{1,2,0:T(8,128)(2,1)} %param.11) | copy-start | bytes 49156
  31.7 12.3 %copy-start.5 = (bf16[1,128,8]{1,2,0:T(8,128)(2,1)S(1)}, bf16[1,128,8]{1,2,0:T(8,128)(2,1)}, u32[]{:S(2)}) copy-start(bf16[1,128,8]{1,2,0:T(8,128)(2,1)} %param.13) | copy-start | bytes 6148
  31.7 12.3 %copy-start.6 = (bf16[1,128]{1,0:T(2,128)(2,1)S(1)}, bf16[1,128]{1,0:T(2,128)(2,1)}, u32[]{:S(2)}) copy-start(bf16[1,128]{1,0:T(2,128)(2,1)} %param.14) | copy-start | bytes 772
  31.7 75.7 %copy-start.3 = (bf16[1,1,21,21]{3,2,1,0:T(8,128)(2,1)S(1)}, bf16[1,1,21,21]{3,2,1,0:T(8,128)(2,1)}, u32[]{:S(2)}) copy-start(bf16[1,1,21,21]{3,2,1,0:T(8,128)(2,1)} %param.12) | copy-start | bytes 2650
  38.6 54.1 %all-to-all-start.2 = ((bf16[64,4,4096]{2,1,0:T(4,128)(2,1)}), bf16[64,4,4096]{2,1,0:T(4,128)(2,1)S(1)}, u32[]{:S(2)}, u32[]{:S(2)}) async-start(bf16[64,4,4096]{2,1,0:T(4,128)(2,1)} %reshape.221), calls=%async_computation.2 | async-start | bytes 4194304 | tf_op jit(solution)/shard_map/all_to_all | solution.py:149
  92.7 56.4 %all-to-all-start = ((bf16[64,4,73]{2,1,0:T(4,128)(2,1)}), bf16[64,4,73]{2,1,0:T(4,128)(2,1)S(1)}, u32[]{:S(2)}, u32[]{:S(2)}) async-start(bf16[64,4,73]{2,1,0:T(4,128)(2,1)} %bitcast.4), calls=%async_computation | async-start | bytes 131072 | tf_op jit(solution)/shard_map/all_to_all | solution.py:150
  107.3 349.0 %reduce-scatter.5.cloned.1.call-start = ((), (), s32[]{:S(2)}) async-start(), calls=%async_computation.6 | async-start | bytes 294912 | tf_op jit(solution)/shard_map/reduce_scatter | solution.py:161
  145.8 3.4 copy-start.1
  410.4 0.7 copy-start
  410.4 0.8 copy-start.2
  411.1 83.0 %reduce-scatter.3.cloned.1.call-start = ((), (), s32[]{:S(2)}) async-start(), calls=%async_computation.5 | async-start | bytes 294912 | tf_op jit(solution)/shard_map/reduce_scatter | solution.py:160
Sparse Core Ops, SparseCore 0:
  411.2 45.0 reduce-scatter.4
  459.3 34.7 reduce-scatter.2
where the time goes:
time: 506 us; the launch traced here: 502 us
  waiting for transfers between devices  138 us (27%)
  local copies, waits for them, and re-layouts  135 us (27%)
  matrix products  91.7 us (18%)
  other arithmetic  42.5 us (8%)
  blocking collectives  38 us (8%)
  starting transfers between devices  37.2 us (7%)
  between operations  14.2 us (3%)
  loops' own time  5.66 us (1%)
    while x640, local copies, waits for them, and re-layouts  88.1 us
    all_to_all x1, waiting for transfers between devices, per_device(): lax.all_to_all(packed_pixels, 'patch', split_axis=0, concat_axis=0, tiled...  47.8 us
    reduce_scatter x1, waiting for transfers between devices, per_device(): lax.psum_scatter(depth_map, 'visit', scatter_dimension=0, tiled=True)  44.5 us
    all_gather x1, blocking collectives, per_device(): full_basis = lax.all_gather(basis[0], 'patch', axis=0, tiled=True)  38 us
    reduce_scatter x1, waiting for transfers between devices, per_device(): lax.psum_scatter(numerator, 'visit', scatter_dimension=0, tiled=True)  37.8 us
    dot_general x32, matrix products, update(): jnp.einsum('nri,nic->rc', row_map, spread, preferred_element_type=jnp.flo...  28.8 us
    reduce_sum x32, other arithmetic, update(): column_weight = jnp.sum(column_map.astype(jnp.float32), axis=2)  27.4 us
    squeeze x32, local copies, waits for them, and re-layouts, accumulate(): final_state, unused = lax.scan(update, initial, blocks)  27.1 us
  transfers between devices with their start and end apart: 5, of which 4 were waited for; matrix products, arithmetic and copies ran while one was open for 2% of the time, Pallas kernels for 0%

commit v1 on v0

v1 whole, which is shorter than its diff:
```python
import functools

import jax
import jax.numpy as jnp
from jax import lax
from jax.experimental import pallas as pl
from jax.experimental.pallas import tpu as pltpu
from jax.sharding import PartitionSpec as P

BF16 = jnp.bfloat16
F32 = jnp.float32
KERNEL = 21
REACH = 10
TERMS = 64
HEIGHT = 32
BREADTH = 128
PATCH = 256
CAP = 4
TAIL = 8
BLOCK_ROWS = CAP * HEIGHT + TAIL
INNER = 3
OUTER = 7
ROWS_T = INNER * HEIGHT
GROUP = 8


def iota(shape, axis):
    return lax.broadcasted_iota(jnp.int32, shape, axis)


def dot(a, b):
    return jnp.dot(a, b, preferred_element_type=F32)


def pack_body(places, target_s, target_row, target_col, stamps, aux, out, count):
    stamp_count = stamps.shape[0]
    out[...] = jnp.zeros_like(out)
    across = target_row[...]
    down = target_col[...]
    square = (stamp_count, stamp_count)
    earlier = (down == across) & (iota(square, 0) < iota(square, 1))
    rank = jnp.sum(jnp.where(earlier, 1, 0), axis=0, keepdims=True)
    row = iota((places * TAIL, stamp_count), 0)
    lane = iota((places * TAIL, stamp_count), 1)
    chosen = jnp.where(row == across * TAIL + (TAIL - CAP) + rank, 1.0, 0.0).astype(BF16)
    part = row & (TAIL - 1)
    shared = jnp.where((lane == part) & (part < TAIL - CAP), 1.0, 0.0).astype(BF16)
    tail = dot(chosen, aux[:stamp_count, :]) + dot(shared, aux[stamp_count:, :])
    out[:, CAP * HEIGHT :, :] = tail.reshape(places, TAIL, BREADTH).astype(BF16)

    def clear(d, carry):
        count[d] = 0
        return carry

    lax.fori_loop(0, places, clear, 0)

    def place(s, carry):
        d = target_s[s]
        k = count[d]
        count[d] = k + 1
        out[d, pl.ds(pl.multiple_of(k * HEIGHT, HEIGHT), HEIGHT), :] = stamps[s]
        return carry

    lax.fori_loop(0, stamp_count, place, 0, unroll=4)


def pack(target, stamps, aux, places):
    stamp_count = stamps.shape[0]
    vmem = pl.BlockSpec(memory_space=pltpu.VMEM)
    return pl.pallas_call(
        functools.partial(pack_body, places),
        out_shape=jax.ShapeDtypeStruct((places, BLOCK_ROWS, BREADTH), BF16),
        in_specs=[pl.BlockSpec(memory_space=pltpu.SMEM), vmem, vmem, vmem, vmem],
        out_specs=vmem,
        scratch_shapes=[pltpu.SMEM((places,), jnp.int32)],
        compiler_params=pltpu.CompilerParams(vmem_limit_bytes=40 << 20),
        name="pack",
    )(target, target[None, :], target[:, None], stamps, aux)


def coadd_body(
    sources, blocks, out, tail, meta, spread_basis, toeplitz, expanded, stack, numer, fields, whole, fields_s, whole_s, sem
):
    slots = CAP * sources
    groups = slots // GROUP
    tail[...] = blocks[:, CAP * HEIGHT :, :].astype(F32).reshape(sources * TAIL, BREADTH)
    basis = jnp.concatenate(
        [tail[pl.ds(q, sources, stride=TAIL), :] for q in range(TAIL - CAP)], axis=1
    ).astype(BF16)
    for k in range(CAP):
        meta[pl.ds(k * sources, sources), :] = tail[pl.ds(TAIL - CAP + k, sources, stride=TAIL), :]
    table = meta[...]
    coefs = table[:, :TERMS].astype(BF16)

    flat = iota((4 * BREADTH, 1), 0)
    a = (flat * 3121) >> 16
    b = flat - a * KERNEL
    outer = (b * 11) >> 5
    there = (b - INNER * outer) * PATCH + outer * HEIGHT + a
    there = jnp.where(flat < KERNEL * KERNEL, there, -1)
    moved = jnp.where(iota((4 * BREADTH, INNER * PATCH), 1) == there, 1.0, 0.0).astype(BF16)
    spread_basis[...] = dot(basis, moved)

    across = iota((TERMS, PATCH), 1) & (HEIGHT - 1)
    for inner in range(INNER):

        def widen(i, carry):
            turned = pltpu.roll(
                spread_basis[:, inner * PATCH : (inner + 1) * PATCH],
                lax.rem(i + (PATCH - REACH), PATCH),
                1,
            )
            near = (across - i <= REACH) & (i - across <= REACH)
            rows = dot(coefs, jnp.where(near, turned, 0.0).astype(BF16))
            at = pl.ds(inner * HEIGHT + i, slots, stride=ROWS_T)
            toeplitz[0, at, :] = rows[:, :BREADTH]
            toeplitz[1, at, :] = rows[:, BREADTH:]
            return carry

        lax.fori_loop(0, HEIGHT, widen, 0)

    turned = table.T
    at = TERMS
    weight = turned[at + 8 : at + 9, :]
    row_start = turned[at + 9 : at + 10, :]
    row_taps = [
        (weight * turned[at + k : at + k + 1, :]).astype(BF16).astype(F32) for k in range(4)
    ]
    fields[...] = jnp.concatenate(
        [turned[at + 4 : at + 8, :], turned[at + 10 : at + 11, :], jnp.zeros((3, slots), F32)], axis=0
    )
    whole[...] = fields[...].astype(jnp.int32)
    copies = [
        pltpu.make_async_copy(fields, fields_s, sem.at[0]),
        pltpu.make_async_copy(whole, whole_s, sem.at[1]),
    ]
    for copy in copies:
        copy.start()

    gap = (iota((PATCH, slots), 0) + 1).astype(F32) - row_start
    row_weight = jnp.zeros((PATCH, slots), F32)
    for k in range(4):
        inside = (gap >= k) & (gap < HEIGHT + k)
        row_weight = row_weight + jnp.where(inside, row_taps[k], 0.0)
    gap = (iota((slots, PATCH), 1) + 1).astype(F32) - table[:, at + 10 : at + 11]
    col_weight = jnp.zeros((slots, PATCH), F32)
    for k in range(4):
        inside = (gap >= k) & (gap < BREADTH + k)
        col_weight = col_weight + jnp.where(inside, table[:, at + 4 + k : at + 5 + k], 0.0)
    row_high = row_weight.astype(BF16)
    row_low = (row_weight - row_high.astype(F32)).astype(BF16)
    col_high = col_weight.astype(BF16)
    col_low = (col_weight - col_high.astype(F32)).astype(BF16)
    depth = dot(row_high, col_high) + (dot(row_high, col_low) + dot(row_low, col_high))
    shares = PATCH // HEIGHT
    for v in range(shares):
        out[v, HEIGHT:, :] = depth[v * HEIGHT : (v + 1) * HEIGHT, :].astype(out.dtype)

    rows = jnp.concatenate(row_taps + [row_start, jnp.zeros((11, slots), F32)], axis=0).astype(BF16)
    owner = iota((slots, GROUP * HEIGHT), 0) - (iota((slots, GROUP * HEIGHT), 1) >> 5)

    def repeat(g, carry):
        hot = jnp.where(owner == g * GROUP, 1.0, 0.0).astype(BF16)
        expanded[g] = dot(rows, hot)
        return carry

    lax.fori_loop(0, groups, repeat, 0)
    for copy in copies:
        copy.wait()

    numer[...] = jnp.zeros_like(numer)
    lane = iota((HEIGHT, BREADTH), 1)
    line = iota((8, BREADTH), 1)
    patch_row = (iota((PATCH, GROUP * HEIGHT), 0) + 1).astype(F32)
    in_stamp = (iota((1, GROUP * HEIGHT), 1) & (HEIGHT - 1)).astype(F32)
    nothing = jnp.zeros((HEIGHT, BREADTH), BF16)
    per_cap = sources // GROUP

    def tall(x):
        return jnp.concatenate([x] * (HEIGHT // 8), axis=0)

    def work(g, carry):
        k = g // per_cap
        first = (g - k * per_cap) * GROUP
        for q in range(GROUP):
            s = g * GROUP + q
            pixels = blocks[first + q, pl.ds(pl.multiple_of(k * HEIGHT, HEIGHT), HEIGHT), :].astype(F32)
            low, high = [], []
            for outer in range(OUTER):
                move = REACH - INNER * outer
                moved = pltpu.roll(pixels, move % BREADTH, 1)
                if move > 0:
                    low.append(jnp.where(lane >= move, moved, 0.0).astype(BF16))
                    if move == 1:
                        moved = jnp.where(lane < move, moved, 0.0)
                    high.append(moved.astype(BF16))
                else:
                    low.append(jnp.where(lane < BREADTH + move, moved, 0.0).astype(BF16))
                    high.append(nothing)
            low.append(nothing)
            high.append(nothing)
            shifted = jnp.concatenate(
                [jnp.concatenate(low, axis=0), jnp.concatenate(high, axis=0)], axis=1
            )
            at = pl.ds(pl.multiple_of(s * ROWS_T, 8), ROWS_T)
            left = jnp.concatenate([toeplitz[0, at, :], toeplitz[1, at, :]], axis=1).astype(BF16)
            product = dot(left, shifted)
            total = product[:HEIGHT, :BREADTH]
            for inner in range(1, INNER):
                part = product[inner * HEIGHT : (inner + 1) * HEIGHT, :]
                total = total + jnp.where(
                    lane < BREADTH - inner,
                    pltpu.roll(part[:, :BREADTH], BREADTH - inner, 1),
                    pltpu.roll(part[:, BREADTH:], BREADTH - inner, 1),
                )
            convolved = total.astype(BF16).astype(F32)
            col_start = whole_s[4, s]
            near, far = [], []
            for t in range(4):
                tap = fields_s[t, s]
                near.append(jnp.where(line >= t, tap, 0.0))
                far.append(jnp.where(line < t, tap, 0.0))
            near[0] = jnp.where((line == 0) & (col_start == 0), 0.0, near[0])
            far[3] = jnp.where((line == 2) & (col_start == BREADTH - 1), 0.0, far[3])
            wide_low = tall(near[0]) * convolved
            wide_high = None
            for t in range(1, 4):
                moved = pltpu.roll(convolved, t, 1)
                wide_low = wide_low + tall(near[t]) * moved
                term = tall(far[t]) * moved
                wide_high = term if wide_high is None else wide_high + term
            wide = jnp.concatenate([wide_low, wide_high], axis=1)
            wide = pltpu.roll(wide, lax.rem(col_start + (PATCH - 1), PATCH), 1)
            stack[pl.ds(q * HEIGHT, HEIGHT), :] = wide.astype(BF16)
        taps = expanded[g]
        gap = patch_row - (taps[4:5, :] + in_stamp)
        row_map = jnp.where(gap == 3.0, taps[3:4, :], 0.0)
        for t in (2, 1, 0):
            row_map = jnp.where(gap == float(t), taps[t : t + 1, :], row_map)
        numer[...] += dot(row_map.astype(BF16), stack[...])
        return carry

    lax.fori_loop(0, groups, work, 0)
    for v in range(shares):
        out[v, :HEIGHT, :] = numer[v * HEIGHT : (v + 1) * HEIGHT, :].astype(out.dtype)


def coadd_sums(blocks):
    sources = blocks.shape[0]
    slots = CAP * sources
    vmem = pl.BlockSpec(memory_space=pltpu.VMEM)
    return pl.pallas_call(
        functools.partial(coadd_body, sources),
        out_shape=jax.ShapeDtypeStruct((PATCH // HEIGHT, 2 * HEIGHT, PATCH), BF16),
        in_specs=[vmem],
        out_specs=vmem,
        scratch_shapes=[
            pltpu.VMEM((sources * TAIL, BREADTH), F32),
            pltpu.VMEM((slots, BREADTH), F32),
            pltpu.VMEM((TERMS, INNER * PATCH), F32),
            pltpu.VMEM((2, slots * ROWS_T, BREADTH), F32),
            pltpu.VMEM((slots // GROUP, 16, GROUP * HEIGHT), F32),
            pltpu.VMEM((GROUP * HEIGHT, PATCH), BF16),
            pltpu.VMEM((PATCH, PATCH), F32),
            pltpu.VMEM((8, slots), F32),
            pltpu.VMEM((8, slots), jnp.int32),
            pltpu.SMEM((8, slots), F32),
            pltpu.SMEM((8, slots), jnp.int32),
            pltpu.SemaphoreType.DMA((2,)),
        ],
        compiler_params=pltpu.CompilerParams(vmem_limit_bytes=48 << 20),
        name="coadd",
    )(blocks)


def per_device(stamps, coefs, basis, taps, weights, target, row_offset, col_offset):
    places = lax.axis_size("patch")
    extras = jnp.concatenate(
        [
            coefs[0],
            taps[0],
            weights[0][:, None],
            row_offset[0].astype(BF16)[:, None],
            col_offset[0].astype(BF16)[:, None],
        ],
        axis=1,
    )
    extras = jnp.pad(extras, ((0, 0), (0, BREADTH - extras.shape[1])))
    flat = jnp.pad(basis.reshape(-1), (0, 4 * BREADTH - KERNEL * KERNEL)).reshape(4, BREADTH)
    aux = jnp.concatenate([extras, jnp.pad(flat, ((0, extras.shape[0] - 4), (0, 0)))], axis=0)
    blocks = pack(target[0, :, 0], stamps[0], aux, places)
    blocks = lax.all_to_all(blocks, "patch", split_axis=0, concat_axis=0, tiled=True)
    sums = coadd_sums(blocks)
    sums = lax.all_to_all(sums, "visit", split_axis=0, concat_axis=0, tiled=True)
    total = jnp.sum(sums.astype(F32), axis=0)
    depth_map = total[HEIGHT:]
    coadd = total[:HEIGHT] / (1.0 + depth_map)
    return (coadd[None], depth_map[None])


def solution(mesh):
    placed = (
        P("visit", "patch", None, None),
        P("visit", "patch", None),
        P("visit", "patch", None, None),
        P("visit", "patch", None),
        P("visit", "patch"),
        P("visit", "patch", None),
        P("visit", "patch"),
        P("visit", "patch"),
    )
    return jax.shard_map(
        per_device,
        mesh=mesh,
        in_specs=placed,
        out_specs=(P("patch", "visit", None), P("patch", "visit", None)),
        check_vma=False,
    )
```

time: 506 us -> 175 us (0.35)
  waiting for transfers between devices: 138 us -> 0 us
  local copies, waits for them, and re-layouts: 135 us -> 6.25 us
  matrix products: 91.7 us -> 0 us
  Pallas kernels: 0 us -> 78.2 us
  blocking collectives: 38 us -> 87.3 us
  other arithmetic: 42.5 us -> 2 us
  starting transfers between devices: 37.2 us -> 0 us
  between operations: 14.2 us -> 0.68 us
  loops' own time: 5.66 us -> 0 us
    dot_general x162 -> x0, matrix products: 91.7 us -> none  [the longest x32 28.8 us: update(): jnp.einsum('nri,nic->rc', row_map, spread, preferred_element_type=jnp.flo...]
    while x640 -> x0, local copies, waits for them, and re-layouts: 88.1 us -> none
    all_to_all x0 -> x2, blocking collectives: none -> 87.3 us  [the longest x1 72.5 us: per_device(): lax.all_to_all(blocks, 'patch', split_axis=0, concat_axis=0, tiled=True)]
    reduce_scatter x2 -> x0, waiting for transfers between devices: 82.3 us -> none  [the longest x1 44.5 us: per_device(): lax.psum_scatter(depth_map, 'visit', scatter_dimension=0, tiled=True)]
    pallas_call x0 -> x2, Pallas kernels: none -> 78.2 us  [the longest x1 76 us: coadd_sums(): pl.pallas_call(functools.partial(coadd_body, sources), out_shape=jax.Shap...]
    all_to_all x3 -> x0, waiting for transfers between devices: 54.7 us -> none  [the longest x1 47.8 us: per_device(): lax.all_to_all(packed_pixels, 'patch', split_axis=0, concat_axis=0, tiled...]
    all_gather x1 -> x0, blocking collectives: 38 us -> none  [per_device(): full_basis = lax.all_gather(basis[0], 'patch', axis=0, tiled=True)]
    all_to_all x3 -> x0, starting transfers between devices: 37.1 us -> none  [the longest x1 17.1 us: per_device(): lax.all_to_all(packed_starts, 'patch', split_axis=0, concat_axis=0, tiled...]
  transfers between devices with their start and end apart: 5 -> 0, of which waited for: 4 -> 0; matrix products, arithmetic and copies ran while one was open for 2% -> 0% of each run, Pallas kernels for 0% -> 0%
where the time goes in v1:
time: 175 us; the launch traced here: 174 us
  blocking collectives  87.3 us (50%)
  Pallas kernels  78.2 us (45%)
  local copies, waits for them, and re-layouts  6.25 us (4%)
  other arithmetic  2 us (1%)
    pallas_call x1, Pallas kernels, coadd_sums(): pl.pallas_call(functools.partial(coadd_body, sources), out_shape=jax.Shap...  76 us
    all_to_all x1, blocking collectives, per_device(): lax.all_to_all(blocks, 'patch', split_axis=0, concat_axis=0, tiled=True)  72.5 us
    all_to_all x1, blocking collectives, per_device(): lax.all_to_all(sums, 'visit', split_axis=0, concat_axis=0, tiled=True)  14.8 us
    unnamed x6, local copies, waits for them, and re-layouts  3.51 us

profile of v1, /device:TPU:1, one launch (start us, length us, event | category | flops | bytes accessed | tf_op | source)
XLA Modules:
  0.0 174.4 jit_solution(507151496046514412)
XLA Ops:
  0.6 0.7 convert_bitcast_fusion.1
  1.3 0.7 convert_bitcast_fusion
  1.9 0.8 reshape.32
  2.7 0.1 copy.14
  2.9 0.1 copy.13
  3.0 0.8 copy.10
  3.9 0.8 copy.11
  4.7 0.8 copy.12
  5.4 0.8 copy.15.target_col
  6.2 0.1 concatenate.6
  6.4 0.0 copy-start
  6.4 1.2 copy-done
  7.6 0.0 copy-start.1
  7.6 0.7 copy-done.1
  8.2 2.2 %pack.1 = bf16[64,136,128]{2,1,0:T(8,128)(2,1)S(1)} custom-call(s32[128]{0:T(128)S(1)} %bitcast.19, s32[1,128]{1,0:T(1,128)S(1)} %bitcast.20, s32[128,1]{1,0:T(8,128)S(1)} %copy.15.target_col, bf16[128,32,128]{2,1,0:T(8,128)(2,1)S(1)} %bitcast.17, bf16[256,128]{1,0:T(8,128)(2,1)S(1)} %fusion.2.aux), custom_call_target="tpu_custom_call" | custom-call | tf_op jit(solution)/shard_map/pack/pallas_call | solution.py:70
  10.4 72.5 %all_to_all.10.blocks = bf16[64,136,128]{2,1,0:T(8,128)(2,1)S(1)} all-to-all(bf16[64,136,128]{2,1,0:T(8,128)(2,1)S(1)} %pack.1), channel_id=1, replica_groups=mesh['patch'=64,'visit'=8] {'patch'}, dimensions={0} | all-to-all | bytes 4456448 | tf_op jit(solution)/shard_map/all_to_all | solution.py:292
  82.9 76.0 %coadd.1 = bf16[8,64,256]{2,1,0:T(8,128)(2,1)S(1)} custom-call(bf16[64,136,128]{2,1,0:T(8,128)(2,1)S(1)} %all_to_all.10.blocks), custom_call_target="tpu_custom_call" | custom-call | tf_op jit(solution)/shard_map/coadd/pallas_call | solution.py:252
  158.9 14.8 %all_to_all.11 = bf16[8,64,256]{2,1,0:T(8,128)(2,1)S(1)} all-to-all(bf16[8,64,256]{2,1,0:T(8,128)(2,1)S(1)} %coadd.1), channel_id=1, replica_groups=mesh['patch'=64,'visit'=8] {'visit'}, dimensions={0} | all-to-all | bytes 524288 | tf_op jit(solution)/shard_map/all_to_all | solution.py:294
  173.7 0.6 slice_bitcast_fusion
  (3 shorter events, 0.1 us)
Async XLA Ops:
  6.4 1.2 copy-start
  7.6 0.7 copy-start.1

commit v2 on v1

v2 whole, which is shorter than its diff:
```python
import functools

import jax
import jax.numpy as jnp
from jax import lax
from jax.experimental import pallas as pl
from jax.experimental.pallas import tpu as pltpu
from jax.sharding import PartitionSpec as P

BF16 = jnp.bfloat16
F32 = jnp.float32
KERNEL = 21
REACH = 10
TERMS = 64
HEIGHT = 32
BREADTH = 128
PATCH = 256
CAP = 4
TAIL = 8
BLOCK_ROWS = CAP * HEIGHT + TAIL
INNER = 3
OUTER = 7
WINDOW = HEIGHT + 8
GROUP = 8
SIDE = 6


def iota(shape, axis):
    return lax.broadcasted_iota(jnp.int32, shape, axis)


def dot(a, b):
    return jnp.dot(a, b, preferred_element_type=F32)


def pack_body(target_s, target, stamps, coefs, basis, taps, weights, row_offset, col_offset, out, held, count, sem):
    places = out.shape[0]
    stamp_count = held.shape[0]
    fetch = pltpu.make_async_copy(stamps, held, sem)
    fetch.start()
    out[...] = jnp.zeros_like(out)
    across = jnp.broadcast_to(target[...].astype(F32), (stamp_count, stamp_count))
    square = (stamp_count, stamp_count)
    earlier = (across.T == across) & (iota(square, 0) < iota(square, 1))
    rank = jnp.sum(jnp.where(earlier, 1.0, 0.0), axis=0, keepdims=True)
    place = target[...] * TAIL + (TAIL - CAP) + rank.astype(jnp.int32)
    chosen = jnp.where(iota((places * TAIL, stamp_count), 0) == place, 1.0, 0.0).astype(BF16)
    extras = jnp.concatenate(
        [
            coefs[...].astype(F32),
            taps[...].astype(F32),
            weights[...].astype(F32),
            row_offset[...].astype(F32),
            col_offset[...].astype(F32),
            jnp.zeros((BREADTH - TERMS - 11, stamp_count), F32),
        ],
        axis=0,
    )
    tail = lax.dot_general(
        chosen, extras.astype(BF16), (((1,), (1,)), ((), ())), preferred_element_type=F32
    )
    wide = jnp.pad(basis[...].astype(F32), ((0, 24 - KERNEL), (0, BREADTH - KERNEL)))
    seat = iota(wide.shape, 0)
    seat = seat - SIDE * ((seat * 11) >> 6)
    laid = jnp.where(seat == 0, wide, 0.0)
    for r in range(1, SIDE):
        laid = laid + jnp.where(seat == r, pltpu.roll(wide, r * KERNEL, 1), 0.0)
    fold = jnp.where((iota((TAIL, 24), 1) * 11) >> 6 == iota((TAIL, 24), 0), 1.0, 0.0)
    shared = dot(fold.astype(BF16), laid.astype(BF16))
    tail = tail.reshape(places, TAIL, BREADTH) + shared[None]
    out[:, CAP * HEIGHT :, :] = tail.astype(BF16)

    def clear(d, carry):
        count[d] = 0
        return carry

    lax.fori_loop(0, places, clear, 0, unroll=8)
    fetch.wait()

    def put(s, carry):
        d = target_s[s]
        k = count[d]
        count[d] = k + 1
        out[d, pl.ds(pl.multiple_of(k * HEIGHT, HEIGHT), HEIGHT), :] = held[s]
        return carry

    lax.fori_loop(0, stamp_count, put, 0, unroll=4)


def pack(target, stamps, coefs, basis, taps, weights, row_offset, col_offset, places):
    vmem = pl.BlockSpec(memory_space=pltpu.VMEM)
    return pl.pallas_call(
        pack_body,
        out_shape=jax.ShapeDtypeStruct((places, BLOCK_ROWS, BREADTH), BF16),
        in_specs=[pl.BlockSpec(memory_space=pltpu.SMEM), vmem, pl.BlockSpec(memory_space=pl.ANY)] + [vmem] * 6,
        out_specs=vmem,
        scratch_shapes=[
            pltpu.VMEM(stamps.shape, BF16),
            pltpu.SMEM((places,), jnp.int32),
            pltpu.SemaphoreType.DMA,
        ],
        compiler_params=pltpu.CompilerParams(vmem_limit_bytes=40 << 20),
        name="pack",
    )(target[0], target, stamps, coefs, basis, taps, weights, row_offset, col_offset)


def coadd_body(sources, blocks, out, tail, meta, kernels, padded, numer, fields, whole, fields_s, whole_s, sem):
    slots = CAP * sources
    groups = slots // GROUP
    tail[...] = blocks[:, CAP * HEIGHT :, :].astype(F32).reshape(sources * TAIL, BREADTH)
    basis = jnp.concatenate(
        [tail[pl.ds(q, sources, stride=TAIL), :] for q in range(TAIL - CAP)], axis=1
    ).astype(BF16)
    for k in range(CAP):
        meta[pl.ds(k * sources, sources), :] = tail[pl.ds(TAIL - CAP + k, sources, stride=TAIL), :]
    table = meta[...]
    coefs = table[:, :TERMS].astype(BF16)

    turned = table.T
    at = TERMS
    weight = turned[at + 8 : at + 9, :]
    row_start = turned[at + 9 : at + 10, :]
    row_taps = [
        (weight * turned[at + k : at + k + 1, :]).astype(BF16).astype(F32) for k in range(4)
    ]
    fields[...] = jnp.concatenate(row_taps + [turned[at + 4 : at + 8, :]], axis=0)
    whole[...] = jnp.concatenate(
        [turned[at + 9 : at + 11, :], jnp.zeros((6, slots), F32)], axis=0
    ).astype(jnp.int32)
    copies = [
        pltpu.make_async_copy(fields, fields_s, sem.at[0]),
        pltpu.make_async_copy(whole, whole_s, sem.at[1]),
    ]
    for copy in copies:
        copy.start()

    flat = iota((4 * BREADTH, 1), 0)
    seat = flat & (BREADTH - 1)
    turn = (seat * 3121) >> 16
    a = (flat >> 7) * SIDE + turn
    b = seat - turn * KERNEL
    outer = (b * 11) >> 5
    there = (b - INNER * outer) * PATCH + (outer >> 2) * BREADTH
    there = there + ((outer * HEIGHT + a - REACH) & (BREADTH - 1))
    there = jnp.where((turn < SIDE) & (a < KERNEL), there, -1)
    moved = jnp.where(iota((4 * BREADTH, INNER * PATCH), 1) == there, 1.0, 0.0).astype(BF16)
    arranged = dot(basis, moved).astype(BF16)
    made = dot(coefs, arranged).astype(BF16).astype(F32)
    for part in range(2 * INNER):
        kernels[part] = made[:, part * BREADTH : (part + 1) * BREADTH]

    gap = (iota((PATCH, slots), 0) + 1).astype(F32) - row_start
    row_weight = jnp.zeros((PATCH, slots), F32)
    for k in range(4):
        inside = (gap >= k) & (gap < HEIGHT + k)
        row_weight = row_weight + jnp.where(inside, row_taps[k], 0.0)
    gap = (iota((slots, PATCH), 1) + 1).astype(F32) - table[:, at + 10 : at + 11]
    col_weight = jnp.zeros((slots, PATCH), F32)
    for k in range(4):
        inside = (gap >= k) & (gap < BREADTH + k)
        col_weight = col_weight + jnp.where(inside, table[:, at + 4 + k : at + 5 + k], 0.0)
    row_high = row_weight.astype(BF16)
    row_low = (row_weight - row_high.astype(F32)).astype(BF16)
    col_high = col_weight.astype(BF16)
    col_low = (col_weight - col_high.astype(F32)).astype(BF16)
    depth = dot(row_high, col_high) + (dot(row_high, col_low) + dot(row_low, col_high))
    shares = PATCH // HEIGHT
    for v in range(shares):
        out[v, HEIGHT:, :] = depth[v * HEIGHT : (v + 1) * HEIGHT, :].astype(out.dtype)

    for copy in copies:
        copy.wait()

    numer[...] = jnp.zeros_like(numer)
    padded[...] = jnp.zeros_like(padded)
    lane = iota((HEIGHT, BREADTH), 1)
    line = iota((8, BREADTH), 1)
    apart = (lane & (HEIGHT - 1)) - iota((HEIGHT, BREADTH), 0)
    near_row = (apart <= REACH) & (apart >= -REACH)
    nothing = jnp.zeros((HEIGHT, BREADTH), BF16)
    per_cap = sources // GROUP

    def tall(x):
        return jnp.concatenate([x] * (WINDOW // 8), axis=0)

    def work(g, carry):
        k = g // per_cap
        first = (g - k * per_cap) * GROUP
        for q in range(GROUP):
            s = g * GROUP + q
            pixels = blocks[first + q, pl.ds(pl.multiple_of(k * HEIGHT, HEIGHT), HEIGHT), :]
            low, high = [], []
            for outer in range(OUTER):
                move = REACH - 1 - INNER * outer
                if move == 0:
                    low.append(pixels)
                    high.append(nothing)
                    continue
                moved = pltpu.roll(pixels.astype(F32), move % BREADTH, 1).astype(BF16)
                kept = lane >= move if move > 0 else lane < BREADTH + move
                low.append(jnp.where(kept, moved, nothing))
                high.append(jnp.where(kept, nothing, moved))
            low.append(nothing)
            high.append(nothing)
            shifted = jnp.concatenate(
                [jnp.concatenate(low, axis=0), jnp.concatenate(high, axis=0)], axis=1
            )
            halves = []
            for half in range(2):
                rows = []
                for inner in range(INNER):
                    row = kernels[2 * inner + half, pl.ds(s, 1), :]
                    turn = pltpu.roll(
                        jnp.broadcast_to(row, (HEIGHT, BREADTH)), 0, 1, stride=1, stride_axis=0
                    )
                    rows.append(jnp.where(near_row, turn, 0.0).astype(BF16))
                halves.append(jnp.concatenate(rows, axis=0))
            left = jnp.concatenate(halves, axis=1)
            product = dot(left, shifted)
            before, centre, after = (product[inner * HEIGHT : (inner + 1) * HEIGHT, :] for inner in range(INNER))
            before = jnp.where(lane == BREADTH - 1, before[:, BREADTH:], before[:, :BREADTH])
            after = jnp.where(lane == 0, after[:, BREADTH:], after[:, :BREADTH])
            total = centre[:, :BREADTH] + pltpu.roll(before, 1, 1) + pltpu.roll(after, BREADTH - 1, 1)
            row_at = whole_s[0, s]
            col_at = whole_s[1, s]
            padded[q, pl.ds(8, HEIGHT), :] = total.astype(BF16).astype(F32)
            tapped = fields_s[0, s] * padded[q, pl.ds(8, WINDOW), :]
            for t in range(1, 4):
                tapped = tapped + fields_s[t, s] * padded[q, pl.ds(8 - t, WINDOW), :]
            wide_low = wide_high = None
            for t in range(4):
                tap = fields_s[4 + t, s]
                start = col_at + (t - 1)
                near = jnp.where(line >= start, tap, 0.0)
                far = jnp.where(line < start, tap, 0.0)
                if t == 0:
                    near = jnp.where((line == BREADTH - 1) & (col_at == 0), 0.0, near)
                if t == 3:
                    far = jnp.where((line == 0) & (col_at == BREADTH - 1), 0.0, far)
                moved = pltpu.roll(tapped, lax.rem(start + BREADTH, BREADTH), 1)
                low_term, high_term = tall(near) * moved, tall(far) * moved
                wide_low = low_term if t == 0 else wide_low + low_term
                wide_high = high_term if t == 0 else wide_high + high_term
            numer[q % 2, 0, pl.ds(row_at + 7, WINDOW), :] += wide_low
            numer[q % 2, 1, pl.ds(row_at + 7, WINDOW), :] += wide_high
        return carry

    lax.fori_loop(0, groups, work, 0)
    for v in range(shares):
        rows = pl.ds(8 + v * HEIGHT, HEIGHT)
        for half in range(2):
            both = numer[0, half, rows, :] + numer[1, half, rows, :]
            out[v, :HEIGHT, half * BREADTH : (half + 1) * BREADTH] = both.astype(out.dtype)


def coadd_sums(blocks):
    sources = blocks.shape[0]
    slots = CAP * sources
    vmem = pl.BlockSpec(memory_space=pltpu.VMEM)
    return pl.pallas_call(
        functools.partial(coadd_body, sources),
        out_shape=jax.ShapeDtypeStruct((PATCH // HEIGHT, 2 * HEIGHT, PATCH), BF16),
        in_specs=[vmem],
        out_specs=vmem,
        scratch_shapes=[
            pltpu.VMEM((sources * TAIL, BREADTH), F32),
            pltpu.VMEM((slots, BREADTH), F32),
            pltpu.VMEM((2 * INNER, slots, BREADTH), F32),
            pltpu.VMEM((GROUP, 8 + HEIGHT + 8, BREADTH), F32),
            pltpu.VMEM((2, 2, PATCH + 16, BREADTH), F32),
            pltpu.VMEM((8, slots), F32),
            pltpu.VMEM((8, slots), jnp.int32),
            pltpu.SMEM((8, slots), F32),
            pltpu.SMEM((8, slots), jnp.int32),
            pltpu.SemaphoreType.DMA((2,)),
        ],
        compiler_params=pltpu.CompilerParams(vmem_limit_bytes=48 << 20),
        name="coadd",
    )(blocks)


def per_device(stamps, coefs, basis, taps, weights, target, row_offset, col_offset):
    places = lax.axis_size("patch")
    blocks = pack(
        target[:, :, 0], stamps[0], coefs[0].T, basis[0, 0], taps[0].T, weights, row_offset, col_offset, places
    )
    blocks = lax.all_to_all(blocks, "patch", split_axis=0, concat_axis=0, tiled=True)
    sums = coadd_sums(blocks)
    sums = lax.all_to_all(sums, "visit", split_axis=0, concat_axis=0, tiled=True)
    total = jnp.sum(sums.astype(F32), axis=0)
    depth_map = total[HEIGHT:]
    coadd = total[:HEIGHT] / (1.0 + depth_map)
    return (coadd[None], depth_map[None])


def solution(mesh):
    placed = (
        P("visit", "patch", None, None),
        P("visit", "patch", None),
        P("visit", "patch", None, None),
        P("visit", "patch", None),
        P("visit", "patch"),
        P("visit", "patch", None),
        P("visit", "patch"),
        P("visit", "patch"),
    )
    return jax.shard_map(
        per_device,
        mesh=mesh,
        in_specs=placed,
        out_specs=(P("patch", "visit", None), P("patch", "visit", None)),
        check_vma=False,
    )
```

time: 175 us -> 119 us (0.68)
  Pallas kernels: 78.2 us -> 24.3 us
    pallas_call x1, Pallas kernels: 76 us -> 22.4 us  [coadd_sums(): pl.pallas_call(functools.partial(coadd_body, sources), out_shape=jax.Shap...]
    unnamed x6 -> x16, local copies, waits for them, and re-layouts: 3.51 us -> 5.93 us
where the time goes in v2:
time: 119 us
  blocking collectives  87.3 us (73%)
  Pallas kernels  24.3 us (20%)
  local copies, waits for them, and re-layouts  5.93 us (5%)
    all_to_all x1, blocking collectives, per_device(): lax.all_to_all(blocks, 'patch', split_axis=0, concat_axis=0, tiled=True)  72.5 us
    pallas_call x1, Pallas kernels, coadd_sums(): pl.pallas_call(functools.partial(coadd_body, sources), out_shape=jax.Shap...  22.4 us
    all_to_all x1, blocking collectives, per_device(): lax.all_to_all(sums, 'visit', split_axis=0, concat_axis=0, tiled=True)  14.8 us
    unnamed x16, local copies, waits for them, and re-layouts  5.93 us

profile of v2, /device:TPU:1, one launch (start us, length us, event | category | flops | bytes accessed | tf_op | source)
XLA Modules:
  0.0 118.8 jit_solution(1036917010363793744)
XLA Ops:
  0.6 0.0 copy-start
  0.6 1.2 %copy-done = bf16[1,128,32,128]{3,2,1,0:T(8,128)(2,1)S(1)} copy-done((bf16[1,128,32,128]{3,2,1,0:T(8,128)(2,1)S(1)}, bf16[1,128,32,128]{3,2,1,0:T(8,128)(2,1)}, u32[]{:S(2)}) %copy-start) | copy-done | bytes 1048600
  1.9 0.0 copy-start.1
  1.9 0.7 copy-done.1
  2.6 0.0 copy-start.2
  2.6 0.7 copy-done.2
  3.3 0.0 copy-start.3
  3.3 0.7 copy-done.3
  4.0 0.0 copy-start.4
  4.0 0.7 copy-done.4
  4.6 0.0 copy-start.5
  4.6 0.7 copy-done.5
  5.3 0.0 copy-start.6
  5.3 0.7 copy-done.6
  5.9 0.0 copy-start.7
  5.9 0.7 copy-done.7
  6.6 1.9 %pack.1 = bf16[64,136,128]{2,1,0:T(8,128)(2,1)S(1)} custom-call(s32[128]{0:T(128)S(1)} %bitcast.18, s32[1,128]{1,0:T(1,128)S(1)} %bitcast.19, bf16[128,32,128]{2,1,0:T(8,128)(2,1)S(1)} %bitcast.14, bf16[64,128]{1,0:T(8,128)(2,1)S(1)} %bitcast.15, bf16[21,21]{1,0:T(8,128)(2,1)S(1)} %bitcast.16, bf16[8,128]{1,0:T(8,128)(2,1)S(1)} %bitcast.17, ...), custom_call_target="tpu_custom_call" | custom-call | tf_op jit(solution)/shard_map/pack/pallas_call | solution.py:92
  8.4 72.5 %all_to_all.10.blocks = bf16[64,136,128]{2,1,0:T(8,128)(2,1)S(1)} all-to-all(bf16[64,136,128]{2,1,0:T(8,128)(2,1)S(1)} %pack.1), channel_id=1, replica_groups=mesh['patch'=64,'visit'=8] {'patch'}, dimensions={0} | all-to-all | bytes 4456448 | tf_op jit(solution)/shard_map/all_to_all | solution.py:287
  80.9 22.4 %coadd.1 = bf16[8,64,256]{2,1,0:T(8,128)(2,1)S(1)} custom-call(bf16[64,136,128]{2,1,0:T(8,128)(2,1)S(1)} %all_to_all.10.blocks), custom_call_target="tpu_custom_call" | custom-call | tf_op jit(solution)/shard_map/coadd/pallas_call | solution.py:260
  103.4 14.8 %all_to_all.11 = bf16[8,64,256]{2,1,0:T(8,128)(2,1)S(1)} all-to-all(bf16[8,64,256]{2,1,0:T(8,128)(2,1)S(1)} %coadd.1), channel_id=1, replica_groups=mesh['patch'=64,'visit'=8] {'visit'}, dimensions={0} | all-to-all | bytes 524288 | tf_op jit(solution)/shard_map/all_to_all | solution.py:289
  118.2 0.6 slice_bitcast_fusion
  (1 shorter events, 0.0 us)
Async XLA Ops:
  0.6 1.2 %copy-start = (bf16[1,128,32,128]{3,2,1,0:T(8,128)(2,1)S(1)}, bf16[1,128,32,128]{3,2,1,0:T(8,128)(2,1)}, u32[]{:S(2)}) copy-start(bf16[1,128,32,128]{3,2,1,0:T(8,128)(2,1)} %param.8) | copy-start | bytes 3145732
  1.9 0.7 copy-start.1
  2.6 0.7 copy-start.2
  3.3 0.7 copy-start.3
  4.0 0.7 copy-start.4
  4.6 0.7 copy-start.5
  5.3 0.7 copy-start.6
  5.9 0.7 copy-start.7

commit v3 on v2

--- a/solution.py
+++ b/solution.py
@@ -22,6 +22,7 @@
 OUTER = 7
 WINDOW = HEIGHT + 8
 GROUP = 8
+OPERANDS = 9
 SIDE = 6
 
 
@@ -33,12 +34,19 @@
     return jnp.dot(a, b, preferred_element_type=F32)
 
 
-def pack_body(target_s, target, stamps, coefs, basis, taps, weights, row_offset, col_offset, out, held, count, sem):
+def pack_body(*refs):
+    given, out, here, count, sem = refs[:OPERANDS], refs[OPERANDS], refs[OPERANDS + 1 : -2], refs[-2], refs[-1]
+    target_s, target, coefs, basis, taps, weights, row_offset, col_offset, held = here
     places = out.shape[0]
     stamp_count = held.shape[0]
-    fetch = pltpu.make_async_copy(stamps, held, sem)
-    fetch.start()
+    fetches = [
+        pltpu.make_async_copy(source, place, sem.at[n]) for n, (source, place) in enumerate(zip(given, here))
+    ]
+    for fetch in fetches:
+        fetch.start()
     out[...] = jnp.zeros_like(out)
+    for fetch in fetches[:-1]:
+        fetch.wait()
     across = jnp.broadcast_to(target[...].astype(F32), (stamp_count, stamp_count))
     square = (stamp_count, stamp_count)
     earlier = (across.T == across) & (iota(square, 0) < iota(square, 1))
@@ -75,10 +83,10 @@
         return carry
 
     lax.fori_loop(0, places, clear, 0, unroll=8)
-    fetch.wait()
+    fetches[-1].wait()
 
     def put(s, carry):
-        d = target_s[s]
+        d = target_s[0, s]
         k = count[d]
         count[d] = k + 1
         out[d, pl.ds(pl.multiple_of(k * HEIGHT, HEIGHT), HEIGHT), :] = held[s]
@@ -88,23 +96,23 @@
 
 
 def pack(target, stamps, coefs, basis, taps, weights, row_offset, col_offset, places):
-    vmem = pl.BlockSpec(memory_space=pltpu.VMEM)
+    given = (target, target, coefs, basis, taps, weights, row_offset, col_offset, stamps)
+    here = [pltpu.SMEM(target.shape, jnp.int32)] + [pltpu.VMEM(x.shape, x.dtype) for x in given[1:]]
     return pl.pallas_call(
         pack_body,
         out_shape=jax.ShapeDtypeStruct((places, BLOCK_ROWS, BREADTH), BF16),
-        in_specs=[pl.BlockSpec(memory_space=pltpu.SMEM), vmem, pl.BlockSpec(memory_space=pl.ANY)] + [vmem] * 6,
-        out_specs=vmem,
-        scratch_shapes=[
-            pltpu.VMEM(stamps.shape, BF16),
-            pltpu.SMEM((places,), jnp.int32),
-            pltpu.SemaphoreType.DMA,
-        ],
+        in_specs=[pl.BlockSpec(memory_space=pltpu.HBM)] * OPERANDS,
+        out_specs=pl.BlockSpec(memory_space=pltpu.VMEM),
+        scratch_shapes=here + [pltpu.SMEM((places,), jnp.int32), pltpu.SemaphoreType.DMA((OPERANDS,))],
         compiler_params=pltpu.CompilerParams(vmem_limit_bytes=40 << 20),
         name="pack",
-    )(target[0], target, stamps, coefs, basis, taps, weights, row_offset, col_offset)
-
-
-def coadd_body(sources, blocks, out, tail, meta, kernels, padded, numer, fields, whole, fields_s, whole_s, sem):
+    )(*(pltpu.with_memory_space_constraint(x, pltpu.HBM) for x in given))
+
+
+def coadd_body(
+    sources, blocks, out, tail, meta, kernels, left_a, left_b, shifted_a, shifted_b, padded_a, padded_b,
+    sum_a, sum_b, sum_c, sum_d, fields, whole, fields_s, whole_s, sem
+):
     slots = CAP * sources
     groups = slots // GROUP
     tail[...] = blocks[:, CAP * HEIGHT :, :].astype(F32).reshape(sources * TAIL, BREADTH)
@@ -171,8 +179,9 @@
     for copy in copies:
         copy.wait()
 
-    numer[...] = jnp.zeros_like(numer)
-    padded[...] = jnp.zeros_like(padded)
+    sums = (sum_a, sum_b, sum_c, sum_d)
+    for ref in sums + (padded_a, padded_b):
+        ref[...] = jnp.zeros_like(ref)
     lane = iota((HEIGHT, BREADTH), 1)
     line = iota((8, BREADTH), 1)
     apart = (lane & (HEIGHT - 1)) - iota((HEIGHT, BREADTH), 0)
@@ -183,47 +192,45 @@
     def tall(x):
         return jnp.concatenate([x] * (WINDOW // 8), axis=0)
 
-    def work(g, carry):
+    def build(g, left, shifted):
         k = g // per_cap
         first = (g - k * per_cap) * GROUP
         for q in range(GROUP):
-            s = g * GROUP + q
             pixels = blocks[first + q, pl.ds(pl.multiple_of(k * HEIGHT, HEIGHT), HEIGHT), :]
-            low, high = [], []
             for outer in range(OUTER):
+                at = pl.ds(outer * HEIGHT, HEIGHT)
                 move = REACH - 1 - INNER * outer
                 if move == 0:
-                    low.append(pixels)
-                    high.append(nothing)
+                    shifted[q, at, :BREADTH] = pixels
                     continue
                 moved = pltpu.roll(pixels.astype(F32), move % BREADTH, 1).astype(BF16)
                 kept = lane >= move if move > 0 else lane < BREADTH + move
-                low.append(jnp.where(kept, moved, nothing))
-                high.append(jnp.where(kept, nothing, moved))
-            low.append(nothing)
-            high.append(nothing)
-            shifted = jnp.concatenate(
-                [jnp.concatenate(low, axis=0), jnp.concatenate(high, axis=0)], axis=1
-            )
-            halves = []
-            for half in range(2):
-                rows = []
-                for inner in range(INNER):
-                    row = kernels[2 * inner + half, pl.ds(s, 1), :]
+                shifted[q, at, :BREADTH] = jnp.where(kept, moved, nothing)
+                shifted[q, at, BREADTH:] = jnp.where(kept, nothing, moved)
+            for inner in range(INNER):
+                for half in range(2):
+                    row = kernels[2 * inner + half, pl.ds(g * GROUP + q, 1), :]
                     turn = pltpu.roll(
                         jnp.broadcast_to(row, (HEIGHT, BREADTH)), 0, 1, stride=1, stride_axis=0
                     )
-                    rows.append(jnp.where(near_row, turn, 0.0).astype(BF16))
-                halves.append(jnp.concatenate(rows, axis=0))
-            left = jnp.concatenate(halves, axis=1)
-            product = dot(left, shifted)
+                    left[q, pl.ds(inner * HEIGHT, HEIGHT), half * BREADTH : (half + 1) * BREADTH] = jnp.where(
+                        near_row, turn, 0.0
+                    ).astype(BF16)
+
+    def convolve(left, shifted, padded):
+        for q in range(GROUP):
+            product = dot(left[q], shifted[q])
             before, centre, after = (product[inner * HEIGHT : (inner + 1) * HEIGHT, :] for inner in range(INNER))
             before = jnp.where(lane == BREADTH - 1, before[:, BREADTH:], before[:, :BREADTH])
             after = jnp.where(lane == 0, after[:, BREADTH:], after[:, :BREADTH])
             total = centre[:, :BREADTH] + pltpu.roll(before, 1, 1) + pltpu.roll(after, BREADTH - 1, 1)
+            padded[q, pl.ds(8, HEIGHT), :] = total.astype(BF16).astype(F32)
+
+    def resample(g, padded):
+        for q in range(GROUP):
+            s = g * GROUP + q
             row_at = whole_s[0, s]
             col_at = whole_s[1, s]
-            padded[q, pl.ds(8, HEIGHT), :] = total.astype(BF16).astype(F32)
             tapped = fields_s[0, s] * padded[q, pl.ds(8, WINDOW), :]
             for t in range(1, 4):
                 tapped = tapped + fields_s[t, s] * padded[q, pl.ds(8 - t, WINDOW), :]
@@ -241,15 +248,30 @@
                 low_term, high_term = tall(near) * moved, tall(far) * moved
                 wide_low = low_term if t == 0 else wide_low + low_term
                 wide_high = high_term if t == 0 else wide_high + high_term
-            numer[q % 2, 0, pl.ds(row_at + 7, WINDOW), :] += wide_low
-            numer[q % 2, 1, pl.ds(row_at + 7, WINDOW), :] += wide_high
+            low, high = sums[2 * (q % 2)], sums[2 * (q % 2) + 1]
+            low[pl.ds(row_at + 7, WINDOW), :] += wide_low
+            high[pl.ds(row_at + 7, WINDOW), :] += wide_high
+
+    for ref in (shifted_a, shifted_b):
+        ref[...] = jnp.zeros_like(ref)
+    build(0, left_a, shifted_a)
+
+    def work(h, carry):
+        g = 2 * h
+        build(g + 1, left_b, shifted_b)
+        convolve(left_a, shifted_a, padded_a)
+        resample(jnp.maximum(g - 1, 0), padded_b)
+        build(jnp.minimum(g + 2, groups - 1), left_a, shifted_a)
+        convolve(left_b, shifted_b, padded_b)
+        resample(g, padded_a)
         return carry
 
-    lax.fori_loop(0, groups, work, 0)
+    lax.fori_loop(0, groups // 2, work, 0)
+    resample(groups - 1, padded_b)
     for v in range(shares):
         rows = pl.ds(8 + v * HEIGHT, HEIGHT)
         for half in range(2):
-            both = numer[0, half, rows, :] + numer[1, half, rows, :]
+            both = sums[half][rows, :] + sums[2 + half][rows, :]
             out[v, :HEIGHT, half * BREADTH : (half + 1) * BREADTH] = both.astype(out.dtype)
 
 
@@ -266,8 +288,16 @@
             pltpu.VMEM((sources * TAIL, BREADTH), F32),
             pltpu.VMEM((slots, BREADTH), F32),
             pltpu.VMEM((2 * INNER, slots, BREADTH), F32),
+            pltpu.VMEM((GROUP, INNER * HEIGHT, PATCH), BF16),
+            pltpu.VMEM((GROUP, INNER * HEIGHT, PATCH), BF16),
+            pltpu.VMEM((GROUP, PATCH, PATCH), BF16),
+            pltpu.VMEM((GROUP, PATCH, PATCH), BF16),
             pltpu.VMEM((GROUP, 8 + HEIGHT + 8, BREADTH), F32),
-            pltpu.VMEM((2, 2, PATCH + 16, BREADTH), F32),
+            pltpu.VMEM((GROUP, 8 + HEIGHT + 8, BREADTH), F32),
+            pltpu.VMEM((PATCH + 16, BREADTH), F32),
+            pltpu.VMEM((PATCH + 16, BREADTH), F32),
+            pltpu.VMEM((PATCH + 16, BREADTH), F32),
+            pltpu.VMEM((PATCH + 16, BREADTH), F32),
             pltpu.VMEM((8, slots), F32),
             pltpu.VMEM((8, slots), jnp.int32),
             pltpu.SMEM((8, slots), F32),

time: 119 us -> 111 us (0.933)
  local copies, waits for them, and re-layouts: 5.93 us -> 0 us
  Pallas kernels: 24.3 us -> 22.2 us
    unnamed x16 -> x0, local copies, waits for them, and re-layouts: 5.93 us -> none
    pallas_call x1, Pallas kernels: 22.4 us -> 20.2 us  [coadd_sums(): pl.pallas_call(functools.partial(coadd_body, sources), out_shape=jax.Shap...]
where the time goes in v3:
time: 111 us
  blocking collectives  87.3 us (79%)
  Pallas kernels  22.2 us (20%)
    all_to_all x1, blocking collectives, per_device(): lax.all_to_all(blocks, 'patch', split_axis=0, concat_axis=0, tiled=True)  72.5 us
    pallas_call x1, Pallas kernels, coadd_sums(): pl.pallas_call(functools.partial(coadd_body, sources), out_shape=jax.Shap...  20.2 us
    all_to_all x1, blocking collectives, per_device(): lax.all_to_all(sums, 'visit', split_axis=0, concat_axis=0, tiled=True)  14.8 us

profile of v3, /device:TPU:1, one launch (start us, length us, event | category | flops | bytes accessed | tf_op | source)
XLA Modules:
  0.0 110.8 jit_solution(8333223539193272673)
XLA Ops:
  0.6 2.1 %pack.1 = bf16[64,136,128]{2,1,0:T(8,128)(2,1)S(1)} custom-call(s32[1,128]{1,0:T(1,128)} %bitcast.17, s32[1,128]{1,0:T(1,128)} %bitcast.18, bf16[64,128]{1,0:T(8,128)(2,1)} %bitcast.14, bf16[21,21]{1,0:T(8,128)(2,1)} %bitcast.15, bf16[8,128]{1,0:T(8,128)(2,1)} %bitcast.16, bf16[1,128]{1,0:T(2,128)(2,1)} %refs_5_.1, s32[1,128]{1,0:T(1,128)} %refs_6_.1, ...), custom_call_target="tpu_custom_call" | custom-call | tf_op jit(solution)/shard_map/pack/pallas_call | solution.py:101
  2.7 72.5 %all_to_all.10.blocks = bf16[64,136,128]{2,1,0:T(8,128)(2,1)S(1)} all-to-all(bf16[64,136,128]{2,1,0:T(8,128)(2,1)S(1)} %pack.1), channel_id=1, replica_groups=mesh['patch'=64,'visit'=8] {'patch'}, dimensions={0} | all-to-all | bytes 4456448 | tf_op jit(solution)/shard_map/all_to_all | solution.py:317
  75.2 20.2 %coadd.1 = bf16[8,64,256]{2,1,0:T(8,128)(2,1)S(1)} custom-call(bf16[64,136,128]{2,1,0:T(8,128)(2,1)S(1)} %all_to_all.10.blocks), custom_call_target="tpu_custom_call" | custom-call | tf_op jit(solution)/shard_map/coadd/pallas_call | solution.py:282
  95.4 14.8 %all_to_all.11 = bf16[8,64,256]{2,1,0:T(8,128)(2,1)S(1)} all-to-all(bf16[8,64,256]{2,1,0:T(8,128)(2,1)S(1)} %coadd.1), channel_id=1, replica_groups=mesh['patch'=64,'visit'=8] {'visit'}, dimensions={0} | all-to-all | bytes 524288 | tf_op jit(solution)/shard_map/all_to_all | solution.py:319
  110.2 0.6 slice_bitcast_fusion
  (1 shorter events, 0.0 us)

commit v4 on v3

--- a/solution.py
+++ b/solution.py
@@ -16,8 +16,9 @@
 BREADTH = 128
 PATCH = 256
 CAP = 4
+EARLY = 3
 TAIL = 8
-BLOCK_ROWS = CAP * HEIGHT + TAIL
+BLOCK_ROWS = EARLY * HEIGHT + TAIL
 INNER = 3
 OUTER = 7
 WINDOW = HEIGHT + 8
@@ -35,7 +36,8 @@
 
 
 def pack_body(*refs):
-    given, out, here, count, sem = refs[:OPERANDS], refs[OPERANDS], refs[OPERANDS + 1 : -2], refs[-2], refs[-1]
+    given, (out, late), here = refs[:OPERANDS], refs[OPERANDS : OPERANDS + 2], refs[OPERANDS + 2 : -2]
+    count, sem = refs[-2], refs[-1]
     target_s, target, coefs, basis, taps, weights, row_offset, col_offset, held = here
     places = out.shape[0]
     stamp_count = held.shape[0]
@@ -45,6 +47,7 @@
     for fetch in fetches:
         fetch.start()
     out[...] = jnp.zeros_like(out)
+    late[...] = jnp.zeros_like(late)
     for fetch in fetches[:-1]:
         fetch.wait()
     across = jnp.broadcast_to(target[...].astype(F32), (stamp_count, stamp_count))
@@ -76,7 +79,7 @@
     fold = jnp.where((iota((TAIL, 24), 1) * 11) >> 6 == iota((TAIL, 24), 0), 1.0, 0.0)
     shared = dot(fold.astype(BF16), laid.astype(BF16))
     tail = tail.reshape(places, TAIL, BREADTH) + shared[None]
-    out[:, CAP * HEIGHT :, :] = tail.astype(BF16)
+    out[:, EARLY * HEIGHT :, :] = tail.astype(BF16)
 
     def clear(d, carry):
         count[d] = 0
@@ -89,7 +92,10 @@
         d = target_s[0, s]
         k = count[d]
         count[d] = k + 1
-        out[d, pl.ds(pl.multiple_of(k * HEIGHT, HEIGHT), HEIGHT), :] = held[s]
+        stamp = held[s]
+        at = pl.ds(pl.multiple_of(jnp.minimum(k, EARLY - 1) * HEIGHT, HEIGHT), HEIGHT)
+        out[d, at, :] = jnp.where(k < EARLY, stamp, out[d, at, :])
+        late[d] = stamp
         return carry
 
     lax.fori_loop(0, stamp_count, put, 0, unroll=4)
@@ -100,94 +106,23 @@
     here = [pltpu.SMEM(target.shape, jnp.int32)] + [pltpu.VMEM(x.shape, x.dtype) for x in given[1:]]
     return pl.pallas_call(
         pack_body,
-        out_shape=jax.ShapeDtypeStruct((places, BLOCK_ROWS, BREADTH), BF16),
+        out_shape=[jax.ShapeDtypeStruct((places, rows, BREADTH), BF16) for rows in (BLOCK_ROWS, HEIGHT)],
         in_specs=[pl.BlockSpec(memory_space=pltpu.HBM)] * OPERANDS,
-        out_specs=pl.BlockSpec(memory_space=pltpu.VMEM),
+        out_specs=[pl.BlockSpec(memory_space=pltpu.VMEM)] * 2,
         scratch_shapes=here + [pltpu.SMEM((places,), jnp.int32), pltpu.SemaphoreType.DMA((OPERANDS,))],
         compiler_params=pltpu.CompilerParams(vmem_limit_bytes=40 << 20),
         name="pack",
     )(*(pltpu.with_memory_space_constraint(x, pltpu.HBM) for x in given))
 
 
-def coadd_body(
-    sources, blocks, out, tail, meta, kernels, left_a, left_b, shifted_a, shifted_b, padded_a, padded_b,
-    sum_a, sum_b, sum_c, sum_d, fields, whole, fields_s, whole_s, sem
-):
-    slots = CAP * sources
-    groups = slots // GROUP
-    tail[...] = blocks[:, CAP * HEIGHT :, :].astype(F32).reshape(sources * TAIL, BREADTH)
-    basis = jnp.concatenate(
-        [tail[pl.ds(q, sources, stride=TAIL), :] for q in range(TAIL - CAP)], axis=1
-    ).astype(BF16)
-    for k in range(CAP):
-        meta[pl.ds(k * sources, sources), :] = tail[pl.ds(TAIL - CAP + k, sources, stride=TAIL), :]
-    table = meta[...]
-    coefs = table[:, :TERMS].astype(BF16)
-
-    turned = table.T
-    at = TERMS
-    weight = turned[at + 8 : at + 9, :]
-    row_start = turned[at + 9 : at + 10, :]
-    row_taps = [
-        (weight * turned[at + k : at + k + 1, :]).astype(BF16).astype(F32) for k in range(4)
-    ]
-    fields[...] = jnp.concatenate(row_taps + [turned[at + 4 : at + 8, :]], axis=0)
-    whole[...] = jnp.concatenate(
-        [turned[at + 9 : at + 11, :], jnp.zeros((6, slots), F32)], axis=0
-    ).astype(jnp.int32)
-    copies = [
-        pltpu.make_async_copy(fields, fields_s, sem.at[0]),
-        pltpu.make_async_copy(whole, whole_s, sem.at[1]),
-    ]
-    for copy in copies:
-        copy.start()
-
-    flat = iota((4 * BREADTH, 1), 0)
-    seat = flat & (BREADTH - 1)
-    turn = (seat * 3121) >> 16
-    a = (flat >> 7) * SIDE + turn
-    b = seat - turn * KERNEL
-    outer = (b * 11) >> 5
-    there = (b - INNER * outer) * PATCH + (outer >> 2) * BREADTH
-    there = there + ((outer * HEIGHT + a - REACH) & (BREADTH - 1))
-    there = jnp.where((turn < SIDE) & (a < KERNEL), there, -1)
-    moved = jnp.where(iota((4 * BREADTH, INNER * PATCH), 1) == there, 1.0, 0.0).astype(BF16)
-    arranged = dot(basis, moved).astype(BF16)
-    made = dot(coefs, arranged).astype(BF16).astype(F32)
-    for part in range(2 * INNER):
-        kernels[part] = made[:, part * BREADTH : (part + 1) * BREADTH]
-
-    gap = (iota((PATCH, slots), 0) + 1).astype(F32) - row_start
-    row_weight = jnp.zeros((PATCH, slots), F32)
-    for k in range(4):
-        inside = (gap >= k) & (gap < HEIGHT + k)
-        row_weight = row_weight + jnp.where(inside, row_taps[k], 0.0)
-    gap = (iota((slots, PATCH), 1) + 1).astype(F32) - table[:, at + 10 : at + 11]
-    col_weight = jnp.zeros((slots, PATCH), F32)
-    for k in range(4):
-        inside = (gap >= k) & (gap < BREADTH + k)
-        col_weight = col_weight + jnp.where(inside, table[:, at + 4 + k : at + 5 + k], 0.0)
-    row_high = row_weight.astype(BF16)
-    row_low = (row_weight - row_high.astype(F32)).astype(BF16)
-    col_high = col_weight.astype(BF16)
-    col_low = (col_weight - col_high.astype(F32)).astype(BF16)
-    depth = dot(row_high, col_high) + (dot(row_high, col_low) + dot(row_low, col_high))
-    shares = PATCH // HEIGHT
-    for v in range(shares):
-        out[v, HEIGHT:, :] = depth[v * HEIGHT : (v + 1) * HEIGHT, :].astype(out.dtype)
-
-    for copy in copies:
-        copy.wait()
-
-    sums = (sum_a, sum_b, sum_c, sum_d)
-    for ref in sums + (padded_a, padded_b):
-        ref[...] = jnp.zeros_like(ref)
+def add_slots(blocks, kernels, fields_s, whole_s, base, groups, sums, buffers):
+    left_a, left_b, shifted_a, shifted_b, padded_a, padded_b = buffers
     lane = iota((HEIGHT, BREADTH), 1)
     line = iota((8, BREADTH), 1)
     apart = (lane & (HEIGHT - 1)) - iota((HEIGHT, BREADTH), 0)
     near_row = (apart <= REACH) & (apart >= -REACH)
     nothing = jnp.zeros((HEIGHT, BREADTH), BF16)
-    per_cap = sources // GROUP
+    per_cap = blocks.shape[0] // GROUP
 
     def tall(x):
         return jnp.concatenate([x] * (WINDOW // 8), axis=0)
@@ -228,7 +163,7 @@
 
     def resample(g, padded):
         for q in range(GROUP):
-            s = g * GROUP + q
+            s = base + g * GROUP + q
             row_at = whole_s[0, s]
             col_at = whole_s[1, s]
             tapped = fields_s[0, s] * padded[q, pl.ds(8, WINDOW), :]
@@ -248,11 +183,11 @@
                 low_term, high_term = tall(near) * moved, tall(far) * moved
                 wide_low = low_term if t == 0 else wide_low + low_term
                 wide_high = high_term if t == 0 else wide_high + high_term
-            low, high = sums[2 * (q % 2)], sums[2 * (q % 2) + 1]
+            low, high = sums.at[2 * (q % 2)], sums.at[2 * (q % 2) + 1]
             low[pl.ds(row_at + 7, WINDOW), :] += wide_low
             high[pl.ds(row_at + 7, WINDOW), :] += wide_high
 
-    for ref in (shifted_a, shifted_b):
+    for ref in (shifted_a, shifted_b, padded_a, padded_b):
         ref[...] = jnp.zeros_like(ref)
     build(0, left_a, shifted_a)
 
@@ -268,54 +203,165 @@
 
     lax.fori_loop(0, groups // 2, work, 0)
     resample(groups - 1, padded_b)
+
+
+def first_body(blocks, sums, late_kernels, fields, whole, depths, tail, meta, kernels, fields_s, whole_s, sem, *buffers):
+    sources = blocks.shape[0]
+    slots = CAP * sources
+    tail[...] = blocks[:, EARLY * HEIGHT :, :].astype(F32).reshape(sources * TAIL, BREADTH)
+    basis = jnp.concatenate(
+        [tail[pl.ds(q, sources, stride=TAIL), :] for q in range(TAIL - CAP)], axis=1
+    ).astype(BF16)
+    for k in range(CAP):
+        meta[pl.ds(k * sources, sources), :] = tail[pl.ds(TAIL - CAP + k, sources, stride=TAIL), :]
+    table = meta[...]
+    coefs = table[:, :TERMS].astype(BF16)
+
+    turned = table.T
+    at = TERMS
+    weight = turned[at + 8 : at + 9, :]
+    row_start = turned[at + 9 : at + 10, :]
+    row_taps = [
+        (weight * turned[at + k : at + k + 1, :]).astype(BF16).astype(F32) for k in range(4)
+    ]
+    fields[...] = jnp.concatenate(row_taps + [turned[at + 4 : at + 8, :]], axis=0)
+    whole[...] = jnp.concatenate(
+        [turned[at + 9 : at + 11, :], jnp.zeros((6, slots), F32)], axis=0
+    ).astype(jnp.int32)
+    copies = [
+        pltpu.make_async_copy(fields, fields_s, sem.at[0]),
+        pltpu.make_async_copy(whole, whole_s, sem.at[1]),
+    ]
+    for copy in copies:
+        copy.start()
+
+    flat = iota((4 * BREADTH, 1), 0)
+    seat = flat & (BREADTH - 1)
+    turn = (seat * 3121) >> 16
+    a = (flat >> 7) * SIDE + turn
+    b = seat - turn * KERNEL
+    outer = (b * 11) >> 5
+    there = (b - INNER * outer) * PATCH + (outer >> 2) * BREADTH
+    there = there + ((outer * HEIGHT + a - REACH) & (BREADTH - 1))
+    there = jnp.where((turn < SIDE) & (a < KERNEL), there, -1)
+    moved = jnp.where(iota((4 * BREADTH, INNER * PATCH), 1) == there, 1.0, 0.0).astype(BF16)
+    arranged = dot(basis, moved).astype(BF16)
+    made = dot(coefs, arranged).astype(BF16).astype(F32)
+    early = EARLY * sources
+    for part in range(2 * INNER):
+        at_part = slice(part * BREADTH, (part + 1) * BREADTH)
+        kernels[part] = made[:early, at_part]
+        late_kernels[part] = made[early:, at_part]
+
+    gap = (iota((PATCH, slots), 0) + 1).astype(F32) - row_start
+    row_weight = jnp.zeros((PATCH, slots), F32)
+    for k in range(4):
+        inside = (gap >= k) & (gap < HEIGHT + k)
+        row_weight = row_weight + jnp.where(inside, row_taps[k], 0.0)
+    gap = (iota((slots, PATCH), 1) + 1).astype(F32) - table[:, at + 10 : at + 11]
+    col_weight = jnp.zeros((slots, PATCH), F32)
+    for k in range(4):
+        inside = (gap >= k) & (gap < BREADTH + k)
+        col_weight = col_weight + jnp.where(inside, table[:, at + 4 + k : at + 5 + k], 0.0)
+    row_high = row_weight.astype(BF16)
+    row_low = (row_weight - row_high.astype(F32)).astype(BF16)
+    col_high = col_weight.astype(BF16)
+    col_low = (col_weight - col_high.astype(F32)).astype(BF16)
+    depth = dot(row_high, col_high) + (dot(row_high, col_low) + dot(row_low, col_high))
+    shares = PATCH // HEIGHT
     for v in range(shares):
+        depths[v] = depth[v * HEIGHT : (v + 1) * HEIGHT, :].astype(depths.dtype)
+
+    sums[...] = jnp.zeros_like(sums)
+    for copy in copies:
+        copy.wait()
+    add_slots(blocks, kernels, fields_s, whole_s, 0, EARLY * sources // GROUP, sums, buffers)
+
+
+def last_body(blocks, before, kernels, fields_s, whole_s, depths, out, sums, *buffers):
+    sources = blocks.shape[0]
+    sums[...] = before[...]
+    add_slots(
+        blocks, kernels, fields_s, whole_s, EARLY * sources, (CAP - EARLY) * sources // GROUP, sums, buffers
+    )
+    for v in range(PATCH // HEIGHT):
         rows = pl.ds(8 + v * HEIGHT, HEIGHT)
         for half in range(2):
-            both = sums[half][rows, :] + sums[2 + half][rows, :]
+            both = sums[half, rows, :] + sums[2 + half, rows, :]
             out[v, :HEIGHT, half * BREADTH : (half + 1) * BREADTH] = both.astype(out.dtype)
-
-
-def coadd_sums(blocks):
+        out[v, HEIGHT:, :] = depths[v]
+
+
+def buffer_shapes():
+    return (
+        [pltpu.VMEM((GROUP, INNER * HEIGHT, PATCH), BF16)] * 2
+        + [pltpu.VMEM((GROUP, PATCH, PATCH), BF16)] * 2
+        + [pltpu.VMEM((GROUP, 8 + HEIGHT + 8, BREADTH), F32)] * 2
+    )
+
+
+def sum_shape():
+    return (4, PATCH + 16, BREADTH)
+
+
+def cost(slots):
+    return pl.CostEstimate(flops=slots * 80_000_000, bytes_accessed=slots * 8192, transcendentals=0)
+
+
+def coadd_first(blocks):
     sources = blocks.shape[0]
     slots = CAP * sources
     vmem = pl.BlockSpec(memory_space=pltpu.VMEM)
     return pl.pallas_call(
-        functools.partial(coadd_body, sources),
-        out_shape=jax.ShapeDtypeStruct((PATCH // HEIGHT, 2 * HEIGHT, PATCH), BF16),
+        first_body,
+        out_shape=[
+            jax.ShapeDtypeStruct(sum_shape(), F32),
+            jax.ShapeDtypeStruct((2 * INNER, slots - EARLY * sources, BREADTH), F32),
+            jax.ShapeDtypeStruct((8, slots), F32),
+            jax.ShapeDtypeStruct((8, slots), jnp.int32),
+            jax.ShapeDtypeStruct((PATCH // HEIGHT, HEIGHT, PATCH), BF16),
+        ],
         in_specs=[vmem],
-        out_specs=vmem,
+        out_specs=[vmem] * 5,
         scratch_shapes=[
             pltpu.VMEM((sources * TAIL, BREADTH), F32),
             pltpu.VMEM((slots, BREADTH), F32),
-            pltpu.VMEM((2 * INNER, slots, BREADTH), F32),
-            pltpu.VMEM((GROUP, INNER * HEIGHT, PATCH), BF16),
-            pltpu.VMEM((GROUP, INNER * HEIGHT, PATCH), BF16),
-            pltpu.VMEM((GROUP, PATCH, PATCH), BF16),
-            pltpu.VMEM((GROUP, PATCH, PATCH), BF16),
-            pltpu.VMEM((GROUP, 8 + HEIGHT + 8, BREADTH), F32),
-            pltpu.VMEM((GROUP, 8 + HEIGHT + 8, BREADTH), F32),
-            pltpu.VMEM((PATCH + 16, BREADTH), F32),
-            pltpu.VMEM((PATCH + 16, BREADTH), F32),
-            pltpu.VMEM((PATCH + 16, BREADTH), F32),
-            pltpu.VMEM((PATCH + 16, BREADTH), F32),
-            pltpu.VMEM((8, slots), F32),
-            pltpu.VMEM((8, slots), jnp.int32),
+            pltpu.VMEM((2 * INNER, EARLY * sources, BREADTH), F32),
             pltpu.SMEM((8, slots), F32),
             pltpu.SMEM((8, slots), jnp.int32),
             pltpu.SemaphoreType.DMA((2,)),
-        ],
-        compiler_params=pltpu.CompilerParams(vmem_limit_bytes=48 << 20),
-        name="coadd",
+        ]
+        + buffer_shapes(),
+        compiler_params=pltpu.CompilerParams(vmem_limit_bytes=40 << 20),
+        cost_estimate=cost(EARLY * sources),
+        name="coadd_first",
     )(blocks)
+
+
+def coadd_last(blocks, before, kernels, fields, whole, depths):
+    vmem = pl.BlockSpec(memory_space=pltpu.VMEM)
+    smem = pl.BlockSpec(memory_space=pltpu.SMEM)
+    return pl.pallas_call(
+        last_body,
+        out_shape=jax.ShapeDtypeStruct((PATCH // HEIGHT, 2 * HEIGHT, PATCH), BF16),
+        in_specs=[vmem, vmem, vmem, smem, smem, vmem],
+        out_specs=vmem,
+        scratch_shapes=[pltpu.VMEM(sum_shape(), F32)] + buffer_shapes(),
+        compiler_params=pltpu.CompilerParams(vmem_limit_bytes=40 << 20),
+        cost_estimate=cost((CAP - EARLY) * blocks.shape[0]),
+        name="coadd_last",
+    )(blocks, before, kernels, fields, whole, depths)
 
 
 def per_device(stamps, coefs, basis, taps, weights, target, row_offset, col_offset):
     places = lax.axis_size("patch")
-    blocks = pack(
+    early, late = pack(
         target[:, :, 0], stamps[0], coefs[0].T, basis[0, 0], taps[0].T, weights, row_offset, col_offset, places
     )
-    blocks = lax.all_to_all(blocks, "patch", split_axis=0, concat_axis=0, tiled=True)
-    sums = coadd_sums(blocks)
+    early = lax.all_to_all(early, "patch", split_axis=0, concat_axis=0, tiled=True)
+    early, late = lax.optimization_barrier((early, late))
+    late = lax.all_to_all(late, "patch", split_axis=0, concat_axis=0, tiled=True)
+    sums = coadd_last(late, *coadd_first(early))
     sums = lax.all_to_all(sums, "visit", split_axis=0, concat_axis=0, tiled=True)
     total = jnp.sum(sums.astype(F32), axis=0)
     depth_map = total[HEIGHT:]

time: 111 us -> 111 us (level)
  blocking collectives: 87.3 us -> 72.4 us
  starting transfers between devices: 0 us -> 12 us
  Pallas kernels: 22.2 us -> 24.7 us
    all_to_all x1, blocking collectives: 72.5 us -> 57.1 us  [per_device(): lax.all_to_all(early, 'patch', split_axis=0, concat_axis=0, tiled=True)]
    all_to_all x0 -> x1, starting transfers between devices: none -> 12 us  [per_device(): lax.all_to_all(late, 'patch', split_axis=0, concat_axis=0, tiled=True)]
    pallas_call x2 -> x3, Pallas kernels: 22.2 us -> 24.7 us  [the longest x1 15.7 us: coadd_first(): pl.pallas_call(first_body, out_shape=[jax.ShapeDtypeStruct(sum_shape(), F...]
  transfers between devices with their start and end apart: 0 -> 1, of which waited for: 0 -> 0; matrix products, arithmetic and copies ran while one was open for 0% -> 0% of each run, Pallas kernels for 0% -> 14%
where the time goes in v4:
time: 111 us
  blocking collectives  72.4 us (65%)
  Pallas kernels  24.7 us (22%)
  starting transfers between devices  12 us (11%)
    all_to_all x1, blocking collectives, per_device(): lax.all_to_all(early, 'patch', split_axis=0, concat_axis=0, tiled=True)  57.1 us
    pallas_call x1, Pallas kernels, coadd_first(): pl.pallas_call(first_body, out_shape=[jax.ShapeDtypeStruct(sum_shape(), F...  15.7 us
    all_to_all x1, blocking collectives, per_device(): lax.all_to_all(sums, 'visit', split_axis=0, concat_axis=0, tiled=True)  15.4 us
    all_to_all x1, starting transfers between devices, per_device(): lax.all_to_all(late, 'patch', split_axis=0, concat_axis=0, tiled=True)  12 us
    pallas_call x1, Pallas kernels, coadd_last(): pl.pallas_call(last_body, out_shape=jax.ShapeDtypeStruct((PATCH // HEIGHT...  5.91 us
    pallas_call x1, Pallas kernels, pack(): pl.pallas_call(pack_body, out_shape=[jax.ShapeDtypeStruct((places, rows,...  3.14 us
  transfers between devices with their start and end apart: 1, of which 0 were waited for; matrix products, arithmetic and copies ran while one was open for 0% of the time, Pallas kernels for 14%

profile of v4, /device:TPU:1, one launch (start us, length us, event | category | flops | bytes accessed | tf_op | source)
XLA Modules:
  0.0 110.5 jit_solution(7907268778916367459)
XLA Ops:
  0.6 3.1 %pack.1 = (bf16[64,104,128]{2,1,0:T(8,128)(2,1)S(1)}, bf16[64,32,128]{2,1,0:T(8,128)(2,1)}) custom-call(s32[1,128]{1,0:T(1,128)} %bitcast.17, s32[1,128]{1,0:T(1,128)} %bitcast.18, bf16[64,128]{1,0:T(8,128)(2,1)} %bitcast.14, bf16[21,21]{1,0:T(8,128)(2,1)} %bitcast.15, bf16[8,128]{1,0:T(8,128)(2,1)} %bitcast.16, bf16[1,128]{1,0:T(2,128)(2,1)} %refs_5_.1, ...), custom_call_target="tpu_custom_call" | custom-call | tf_op jit(solution)/shard_map/pack/pallas_call | solution.py:107
  3.8 57.1 %all_to_all.15.blocks = bf16[64,104,128]{2,1,0:T(8,128)(2,1)S(1)} all-to-all(bf16[64,104,128]{2,1,0:T(8,128)(2,1)S(1)} %get-tuple-element.11), channel_id=1, replica_groups=mesh['patch'=64,'visit'=8] {'patch'}, dimensions={0} | all-to-all | bytes 3407872 | tf_op jit(solution)/shard_map/all_to_all | solution.py:361
  60.9 12.0 %all-to-all-start.1 = ((bf16[64,32,128]{2,1,0:T(8,128)(2,1)}), bf16[64,32,128]{2,1,0:T(8,128)(2,1)S(1)}, u32[]{:S(2)}, u32[]{:S(2)}) async-start(bf16[64,32,128]{2,1,0:T(8,128)(2,1)} %get-tuple-element.13), calls=%async_computation.1 | async-start | bytes 1048576 | tf_op jit(solution)/shard_map/all_to_all | solution.py:363
  72.8 15.7 %coadd_first.1 = (f32[4,272,128]{2,1,0:T(8,128)S(1)}, f32[6,64,128]{2,1,0:T(8,128)S(1)}, f32[8,256]{1,0:T(8,128)S(1)}, s32[8,256]{1,0:T(8,128)S(1)}, bf16[8,32,256]{2,1,0:T(8,128)(2,1)S(1)}) custom-call(bf16[64,104,128]{2,1,0:T(8,128)(2,1)S(1)} %all_to_all.15.blocks), custom_call_target="tpu_custom_call" | custom-call | flops 15360000000 | bytes 1572864 | tf_op jit(solution)/shard_map/coadd_first/pallas_call | solution.py:315
  88.5 0.0 all-to-all-done.1.blocks
  88.6 5.9 %coadd_last.1 = bf16[8,64,256]{2,1,0:T(8,128)(2,1)S(1)} custom-call(bf16[64,32,128]{2,1,0:T(8,128)(2,1)S(1)} %all-to-all-done.1.blocks, f32[4,272,128]{2,1,0:T(8,128)S(1)} %get-tuple-element.15.before, f32[6,64,128]{2,1,0:T(8,128)S(1)} %get-tuple-element.16.kernels, f32[8,256]{1,0:T(8,128)S(1)} %get-tuple-element.17.fields_s, ...), custom_call_target="tpu_custom_call" | custom-call | flops 5120000000 | bytes 524288 | tf_op jit(solution)/shard_map/coadd_last/pallas_call | solution.py:344
  94.5 15.4 %all_to_all.16 = bf16[8,64,256]{2,1,0:T(8,128)(2,1)S(1)} all-to-all(bf16[8,64,256]{2,1,0:T(8,128)(2,1)S(1)} %coadd_last.1), channel_id=1, replica_groups=mesh['patch'=64,'visit'=8] {'visit'}, dimensions={0} | all-to-all | bytes 524288 | tf_op jit(solution)/shard_map/all_to_all | solution.py:365
  109.9 0.6 slice_bitcast_fusion
  (1 shorter events, 0.0 us)
Async XLA Ops:
  60.9 27.7 %all-to-all-start.1 = ((bf16[64,32,128]{2,1,0:T(8,128)(2,1)}), bf16[64,32,128]{2,1,0:T(8,128)(2,1)S(1)}, u32[]{:S(2)}, u32[]{:S(2)}) async-start(bf16[64,32,128]{2,1,0:T(8,128)(2,1)} %get-tuple-element.13), calls=%async_computation.1 | async-start | bytes 1048576 | tf_op jit(solution)/shard_map/all_to_all | solution.py:363

commit v5 on v3

--- a/solution.py
+++ b/solution.py
@@ -192,82 +192,84 @@
     def tall(x):
         return jnp.concatenate([x] * (WINDOW // 8), axis=0)
 
-    def build(g, left, shifted):
+    def build(g, q, left, shifted):
         k = g // per_cap
         first = (g - k * per_cap) * GROUP
-        for q in range(GROUP):
-            pixels = blocks[first + q, pl.ds(pl.multiple_of(k * HEIGHT, HEIGHT), HEIGHT), :]
-            for outer in range(OUTER):
-                at = pl.ds(outer * HEIGHT, HEIGHT)
-                move = REACH - 1 - INNER * outer
-                if move == 0:
-                    shifted[q, at, :BREADTH] = pixels
-                    continue
-                moved = pltpu.roll(pixels.astype(F32), move % BREADTH, 1).astype(BF16)
-                kept = lane >= move if move > 0 else lane < BREADTH + move
-                shifted[q, at, :BREADTH] = jnp.where(kept, moved, nothing)
-                shifted[q, at, BREADTH:] = jnp.where(kept, nothing, moved)
-            for inner in range(INNER):
-                for half in range(2):
-                    row = kernels[2 * inner + half, pl.ds(g * GROUP + q, 1), :]
-                    turn = pltpu.roll(
-                        jnp.broadcast_to(row, (HEIGHT, BREADTH)), 0, 1, stride=1, stride_axis=0
-                    )
-                    left[q, pl.ds(inner * HEIGHT, HEIGHT), half * BREADTH : (half + 1) * BREADTH] = jnp.where(
-                        near_row, turn, 0.0
-                    ).astype(BF16)
-
-    def convolve(left, shifted, padded):
-        for q in range(GROUP):
-            product = dot(left[q], shifted[q])
-            before, centre, after = (product[inner * HEIGHT : (inner + 1) * HEIGHT, :] for inner in range(INNER))
-            before = jnp.where(lane == BREADTH - 1, before[:, BREADTH:], before[:, :BREADTH])
-            after = jnp.where(lane == 0, after[:, BREADTH:], after[:, :BREADTH])
-            total = centre[:, :BREADTH] + pltpu.roll(before, 1, 1) + pltpu.roll(after, BREADTH - 1, 1)
-            padded[q, pl.ds(8, HEIGHT), :] = total.astype(BF16).astype(F32)
-
-    def resample(g, padded):
-        for q in range(GROUP):
-            s = g * GROUP + q
-            row_at = whole_s[0, s]
-            col_at = whole_s[1, s]
-            tapped = fields_s[0, s] * padded[q, pl.ds(8, WINDOW), :]
-            for t in range(1, 4):
-                tapped = tapped + fields_s[t, s] * padded[q, pl.ds(8 - t, WINDOW), :]
-            wide_low = wide_high = None
-            for t in range(4):
-                tap = fields_s[4 + t, s]
-                start = col_at + (t - 1)
-                near = jnp.where(line >= start, tap, 0.0)
-                far = jnp.where(line < start, tap, 0.0)
-                if t == 0:
-                    near = jnp.where((line == BREADTH - 1) & (col_at == 0), 0.0, near)
-                if t == 3:
-                    far = jnp.where((line == 0) & (col_at == BREADTH - 1), 0.0, far)
-                moved = pltpu.roll(tapped, lax.rem(start + BREADTH, BREADTH), 1)
-                low_term, high_term = tall(near) * moved, tall(far) * moved
-                wide_low = low_term if t == 0 else wide_low + low_term
-                wide_high = high_term if t == 0 else wide_high + high_term
-            low, high = sums[2 * (q % 2)], sums[2 * (q % 2) + 1]
-            low[pl.ds(row_at + 7, WINDOW), :] += wide_low
-            high[pl.ds(row_at + 7, WINDOW), :] += wide_high
-
+        pixels = blocks[first + q, pl.ds(pl.multiple_of(k * HEIGHT, HEIGHT), HEIGHT), :]
+        for outer in range(OUTER):
+            at = pl.ds(outer * HEIGHT, HEIGHT)
+            move = REACH - 1 - INNER * outer
+            if move == 0:
+                shifted[q, at, :BREADTH] = pixels
+                continue
+            moved = pltpu.roll(pixels, move % BREADTH, 1)
+            kept = lane >= move if move > 0 else lane < BREADTH + move
+            shifted[q, at, :BREADTH] = jnp.where(kept, moved, nothing)
+            shifted[q, at, BREADTH:] = jnp.where(kept, nothing, moved)
+        for inner in range(INNER):
+            for half in range(2):
+                row = kernels[2 * inner + half, pl.ds(g * GROUP + q, 1), :]
+                turn = pltpu.roll(
+                    jnp.broadcast_to(row, (HEIGHT, BREADTH)), 0, 1, stride=1, stride_axis=0
+                )
+                left[q, pl.ds(inner * HEIGHT, HEIGHT), half * BREADTH : (half + 1) * BREADTH] = jnp.where(
+                    near_row, turn, 0.0
+                ).astype(BF16)
+
+    def convolve(q, left, shifted, padded):
+        product = dot(left[q], shifted[q])
+        before, centre, after = (product[inner * HEIGHT : (inner + 1) * HEIGHT, :] for inner in range(INNER))
+        before = jnp.where(lane == BREADTH - 1, before[:, BREADTH:], before[:, :BREADTH])
+        after = jnp.where(lane == 0, after[:, BREADTH:], after[:, :BREADTH])
+        total = centre[:, :BREADTH] + pltpu.roll(before, 1, 1) + pltpu.roll(after, BREADTH - 1, 1)
+        padded[q, pl.ds(8, HEIGHT), :] = total.astype(BF16).astype(F32)
+
+    def resample(g, q, padded):
+        s = g * GROUP + q
+        row_at = whole_s[0, s]
+        col_at = whole_s[1, s]
+        tapped = fields_s[0, s] * padded[q, pl.ds(8, WINDOW), :]
+        for t in range(1, 4):
+            tapped = tapped + fields_s[t, s] * padded[q, pl.ds(8 - t, WINDOW), :]
+        wide_low = wide_all = None
+        for t in range(4):
+            tap = fields_s[4 + t, s]
+            if t == 0:
+                tap = tall(jnp.where((line == BREADTH - 1) & (col_at == 0), 0.0, tap))
+            if t == 3:
+                tap = tall(jnp.where((line == 0) & (col_at == BREADTH - 1), 0.0, tap))
+            term = tap * pltpu.roll(tapped, lax.rem(col_at + (BREADTH + t - 1), BREADTH), 1)
+            wide_all = term if t == 0 else wide_all + term
+            begun = tall(line >= col_at + (t - 1))
+            wide_low = jnp.where(begun, wide_all, 0.0 if t == 0 else wide_low)
+        wide_high = wide_all - wide_low
+        low, high = sums[2 * (q % 2)], sums[2 * (q % 2) + 1]
+        low[pl.ds(row_at + 7, WINDOW), :] += wide_low
+        high[pl.ds(row_at + 7, WINDOW), :] += wide_high
+
+    used = OUTER * HEIGHT
+    still = pl.ds((OUTER // 2) * HEIGHT, HEIGHT)
     for ref in (shifted_a, shifted_b):
-        ref[...] = jnp.zeros_like(ref)
-    build(0, left_a, shifted_a)
+        ref[:, used:, :] = jnp.zeros((GROUP, PATCH - used, PATCH), BF16)
+        ref[:, still, BREADTH:] = jnp.zeros((GROUP, HEIGHT, BREADTH), BF16)
+    for q in range(GROUP):
+        build(0, q, left_a, shifted_a)
 
     def work(h, carry):
         g = 2 * h
-        build(g + 1, left_b, shifted_b)
-        convolve(left_a, shifted_a, padded_a)
-        resample(jnp.maximum(g - 1, 0), padded_b)
-        build(jnp.minimum(g + 2, groups - 1), left_a, shifted_a)
-        convolve(left_b, shifted_b, padded_b)
-        resample(g, padded_a)
+        for q in range(GROUP):
+            convolve(q, left_a, shifted_a, padded_a)
+            build(g + 1, q, left_b, shifted_b)
+            resample(jnp.maximum(g - 1, 0), q, padded_b)
+        for q in range(GROUP):
+            convolve(q, left_b, shifted_b, padded_b)
+            build(jnp.minimum(g + 2, groups - 1), q, left_a, shifted_a)
+            resample(g, q, padded_a)
         return carry
 
     lax.fori_loop(0, groups // 2, work, 0)
-    resample(groups - 1, padded_b)
+    for q in range(GROUP):
+        resample(groups - 1, q, padded_b)
     for v in range(shares):
         rows = pl.ds(8 + v * HEIGHT, HEIGHT)
         for half in range(2):
@@ -309,6 +311,27 @@
     )(blocks)
 
 
+def finish_body(sums, coadd, depth_map):
+    total = sums[0].astype(F32)
+    for v in range(1, sums.shape[0]):
+        total = total + sums[v].astype(F32)
+    depth = total[HEIGHT:, :]
+    depth_map[...] = depth
+    coadd[...] = total[:HEIGHT, :] / (1.0 + depth)
+
+
+def finish(sums):
+    vmem = pl.BlockSpec(memory_space=pltpu.VMEM)
+    return pl.pallas_call(
+        finish_body,
+        out_shape=[jax.ShapeDtypeStruct((HEIGHT, PATCH), F32)] * 2,
+        in_specs=[vmem],
+        out_specs=[vmem, vmem],
+        compiler_params=pltpu.CompilerParams(vmem_limit_bytes=4 << 20),
+        name="finish",
+    )(sums)
+
+
 def per_device(stamps, coefs, basis, taps, weights, target, row_offset, col_offset):
     places = lax.axis_size("patch")
     blocks = pack(
@@ -317,9 +340,7 @@
     blocks = lax.all_to_all(blocks, "patch", split_axis=0, concat_axis=0, tiled=True)
     sums = coadd_sums(blocks)
     sums = lax.all_to_all(sums, "visit", split_axis=0, concat_axis=0, tiled=True)
-    total = jnp.sum(sums.astype(F32), axis=0)
-    depth_map = total[HEIGHT:]
-    coadd = total[:HEIGHT] / (1.0 + depth_map)
+    coadd, depth_map = finish(sums)
     return (coadd[None], depth_map[None])
 
 

time: 111 us -> 110 us (level)
  no operation moved by 1% of the time
where the time goes in v5:
time: 110 us
  blocking collectives  87.3 us (79%)
  Pallas kernels  22.1 us (20%)
    all_to_all x1, blocking collectives, per_device(): lax.all_to_all(blocks, 'patch', split_axis=0, concat_axis=0, tiled=True)  72.5 us
    pallas_call x1, Pallas kernels, coadd_sums(): pl.pallas_call(functools.partial(coadd_body, sources), out_shape=jax.Shap...  19.4 us
    all_to_all x1, blocking collectives, per_device(): lax.all_to_all(sums, 'visit', split_axis=0, concat_axis=0, tiled=True)  14.8 us

profile of v5, /device:TPU:1, one launch (start us, length us, event | category | flops | bytes accessed | tf_op | source)
XLA Modules:
  0.0 110.1 jit_solution(5527012604947588127)
XLA Ops:
  0.6 2.1 %pack.1 = bf16[64,136,128]{2,1,0:T(8,128)(2,1)S(1)} custom-call(s32[1,128]{1,0:T(1,128)} %bitcast.15, s32[1,128]{1,0:T(1,128)} %bitcast.16, bf16[64,128]{1,0:T(8,128)(2,1)} %bitcast.12, bf16[21,21]{1,0:T(8,128)(2,1)} %bitcast.13, bf16[8,128]{1,0:T(8,128)(2,1)} %bitcast.14, bf16[1,128]{1,0:T(2,128)(2,1)} %refs_5_.1, s32[1,128]{1,0:T(1,128)} %refs_6_.1, ...), custom_call_target="tpu_custom_call" | custom-call | tf_op jit(solution)/shard_map/pack/pallas_call | solution.py:101
  2.7 72.5 %all_to_all.10.blocks = bf16[64,136,128]{2,1,0:T(8,128)(2,1)S(1)} all-to-all(bf16[64,136,128]{2,1,0:T(8,128)(2,1)S(1)} %pack.1), channel_id=1, replica_groups=mesh['patch'=64,'visit'=8] {'patch'}, dimensions={0} | all-to-all | bytes 4456448 | tf_op jit(solution)/shard_map/all_to_all | solution.py:340
  75.2 19.4 %coadd.1 = bf16[8,64,256]{2,1,0:T(8,128)(2,1)S(1)} custom-call(bf16[64,136,128]{2,1,0:T(8,128)(2,1)S(1)} %all_to_all.10.blocks), custom_call_target="tpu_custom_call" | custom-call | tf_op jit(solution)/shard_map/coadd/pallas_call | solution.py:284
  94.6 14.8 %all_to_all.11.sums = bf16[8,64,256]{2,1,0:T(8,128)(2,1)S(1)} all-to-all(bf16[8,64,256]{2,1,0:T(8,128)(2,1)S(1)} %coadd.1), channel_id=1, replica_groups=mesh['patch'=64,'visit'=8] {'visit'}, dimensions={0} | all-to-all | bytes 524288 | tf_op jit(solution)/shard_map/all_to_all | solution.py:342
  109.4 0.7 finish.1

commit v6 on v5

--- a/solution.py
+++ b/solution.py
@@ -111,10 +111,10 @@
 
 def coadd_body(
     sources, blocks, out, tail, meta, kernels, left_a, left_b, shifted_a, shifted_b, padded_a, padded_b,
-    sum_a, sum_b, sum_c, sum_d, fields, whole, fields_s, whole_s, sem
+    sum_a, sum_b, sum_c, sum_d, fields, whole, fields_s, whole_s, listed, sem
 ):
     slots = CAP * sources
-    groups = slots // GROUP
+    bits = sources.bit_length() - 1
     tail[...] = blocks[:, CAP * HEIGHT :, :].astype(F32).reshape(sources * TAIL, BREADTH)
     basis = jnp.concatenate(
         [tail[pl.ds(q, sources, stride=TAIL), :] for q in range(TAIL - CAP)], axis=1
@@ -133,7 +133,7 @@
     ]
     fields[...] = jnp.concatenate(row_taps + [turned[at + 4 : at + 8, :]], axis=0)
     whole[...] = jnp.concatenate(
-        [turned[at + 9 : at + 11, :], jnp.zeros((6, slots), F32)], axis=0
+        [turned[at + 9 : at + 11, :], jnp.where(weight != 0.0, 1.0, 0.0), jnp.zeros((5, slots), F32)], axis=0
     ).astype(jnp.int32)
     copies = [
         pltpu.make_async_copy(fields, fields_s, sem.at[0]),
@@ -187,15 +187,14 @@
     apart = (lane & (HEIGHT - 1)) - iota((HEIGHT, BREADTH), 0)
     near_row = (apart <= REACH) & (apart >= -REACH)
     nothing = jnp.zeros((HEIGHT, BREADTH), BF16)
-    per_cap = sources // GROUP
 
     def tall(x):
         return jnp.concatenate([x] * (WINDOW // 8), axis=0)
 
     def build(g, q, left, shifted):
-        k = g // per_cap
-        first = (g - k * per_cap) * GROUP
-        pixels = blocks[first + q, pl.ds(pl.multiple_of(k * HEIGHT, HEIGHT), HEIGHT), :]
+        s = listed[g * GROUP + q]
+        k = s >> bits
+        pixels = blocks[s - (k << bits), pl.ds(pl.multiple_of(k * HEIGHT, HEIGHT), HEIGHT), :]
         for outer in range(OUTER):
             at = pl.ds(outer * HEIGHT, HEIGHT)
             move = REACH - 1 - INNER * outer
@@ -208,7 +207,7 @@
             shifted[q, at, BREADTH:] = jnp.where(kept, nothing, moved)
         for inner in range(INNER):
             for half in range(2):
-                row = kernels[2 * inner + half, pl.ds(g * GROUP + q, 1), :]
+                row = kernels[2 * inner + half, pl.ds(s, 1), :]
                 turn = pltpu.roll(
                     jnp.broadcast_to(row, (HEIGHT, BREADTH)), 0, 1, stride=1, stride_axis=0
                 )
@@ -225,7 +224,7 @@
         padded[q, pl.ds(8, HEIGHT), :] = total.astype(BF16).astype(F32)
 
     def resample(g, q, padded):
-        s = g * GROUP + q
+        s = listed[g * GROUP + q]
         row_at = whole_s[0, s]
         col_at = whole_s[1, s]
         tapped = fields_s[0, s] * padded[q, pl.ds(8, WINDOW), :]
@@ -252,6 +251,21 @@
     for ref in (shifted_a, shifted_b):
         ref[:, used:, :] = jnp.zeros((GROUP, PATCH - used, PATCH), BF16)
         ref[:, still, BREADTH:] = jnp.zeros((GROUP, HEIGHT, BREADTH), BF16)
+    def note(s, carry):
+        number, empty = carry
+        holds = whole_s[2, s]
+        listed[number] = s
+        return number + holds, jnp.where(holds == 0, s, empty)
+
+    number, empty = lax.fori_loop(0, slots, note, (0, 0), unroll=16)
+
+    def fill(n, carry):
+        listed[number + n] = empty
+        return carry
+
+    lax.fori_loop(0, 2 * GROUP, fill, 0, unroll=4)
+    rounds = jnp.maximum((number + 2 * GROUP - 1) // (2 * GROUP), 1)
+    groups = 2 * rounds
     for q in range(GROUP):
         build(0, q, left_a, shifted_a)
 
@@ -267,7 +281,7 @@
             resample(g, q, padded_a)
         return carry
 
-    lax.fori_loop(0, groups // 2, work, 0)
+    lax.fori_loop(0, rounds, work, 0)
     for q in range(GROUP):
         resample(groups - 1, q, padded_b)
     for v in range(shares):
@@ -304,6 +318,7 @@
             pltpu.VMEM((8, slots), jnp.int32),
             pltpu.SMEM((8, slots), F32),
             pltpu.SMEM((8, slots), jnp.int32),
+            pltpu.SMEM((slots + 2 * GROUP,), jnp.int32),
             pltpu.SemaphoreType.DMA((2,)),
         ],
         compiler_params=pltpu.CompilerParams(vmem_limit_bytes=48 << 20),

time: 110 us -> 104 us (0.945)
  Pallas kernels: 22.1 us -> 15.7 us
    pallas_call x1, Pallas kernels: 19.4 us -> 12.9 us  [coadd_sums(): pl.pallas_call(functools.partial(coadd_body, sources), out_shape=jax.Shap...]
where the time goes in v6:
time: 104 us; the launch traced here: 103 us
  blocking collectives  87 us (84%)
  Pallas kernels  15.7 us (15%)
    all_to_all x1, blocking collectives, per_device(): lax.all_to_all(blocks, 'patch', split_axis=0, concat_axis=0, tiled=True)  72.5 us
    all_to_all x1, blocking collectives, per_device(): lax.all_to_all(sums, 'visit', split_axis=0, concat_axis=0, tiled=True)  14.5 us
    pallas_call x1, Pallas kernels, coadd_sums(): pl.pallas_call(functools.partial(coadd_body, sources), out_shape=jax.Shap...  12.9 us

profile of v6, /device:TPU:1, one launch (start us, length us, event | category | flops | bytes accessed | tf_op | source)
XLA Modules:
  0.0 103.3 jit_solution(14723643592570674230)
XLA Ops:
  0.6 2.1 %pack.1 = bf16[64,136,128]{2,1,0:T(8,128)(2,1)S(1)} custom-call(s32[1,128]{1,0:T(1,128)} %bitcast.15, s32[1,128]{1,0:T(1,128)} %bitcast.16, bf16[64,128]{1,0:T(8,128)(2,1)} %bitcast.12, bf16[21,21]{1,0:T(8,128)(2,1)} %bitcast.13, bf16[8,128]{1,0:T(8,128)(2,1)} %bitcast.14, bf16[1,128]{1,0:T(2,128)(2,1)} %refs_5_.1, s32[1,128]{1,0:T(1,128)} %refs_6_.1, ...), custom_call_target="tpu_custom_call" | custom-call | tf_op jit(solution)/shard_map/pack/pallas_call | solution.py:101
  2.7 72.5 %all_to_all.10.blocks = bf16[64,136,128]{2,1,0:T(8,128)(2,1)S(1)} all-to-all(bf16[64,136,128]{2,1,0:T(8,128)(2,1)S(1)} %pack.1), channel_id=1, replica_groups=mesh['patch'=64,'visit'=8] {'patch'}, dimensions={0} | all-to-all | bytes 4456448 | tf_op jit(solution)/shard_map/all_to_all | solution.py:355
  75.2 12.9 %coadd.1 = bf16[8,64,256]{2,1,0:T(8,128)(2,1)S(1)} custom-call(bf16[64,136,128]{2,1,0:T(8,128)(2,1)S(1)} %all_to_all.10.blocks), custom_call_target="tpu_custom_call" | custom-call | tf_op jit(solution)/shard_map/coadd/pallas_call | solution.py:298
  88.2 14.5 %all_to_all.11.sums = bf16[8,64,256]{2,1,0:T(8,128)(2,1)S(1)} all-to-all(bf16[8,64,256]{2,1,0:T(8,128)(2,1)S(1)} %coadd.1), channel_id=1, replica_groups=mesh['patch'=64,'visit'=8] {'visit'}, dimensions={0} | all-to-all | bytes 524288 | tf_op jit(solution)/shard_map/all_to_all | solution.py:357
  102.7 0.7 finish.1
